TPU v7x, 32 devices: a whole 2x2x4 slice. The times are simulated.
32 devices in a mesh: groups: 2 (over y), nodes: 4 (over z), heads: 2 (over x), sub: 2 (over core).
Axes of the slice: x: 2, y: 2, z: 4, core: 2. Of those that a mesh axis runs over, the one named last changes fastest.
Arguments:
- queries: bfloat16 [4096, 512], P(('groups', 'nodes', 'sub'), 'heads'), parts along dimension 0, may hold values from -60 to 60
- key_vectors: bfloat16 [4096, 512], P(('groups', 'nodes', 'sub'), 'heads'), parts along dimension 0, may hold values from -20 to 20
- value_vectors: bfloat16 [4096, 512], P(('groups', 'nodes', 'sub'), 'heads'), parts along dimension 0, may hold values from -6 to 6
- cotangent: bfloat16 [4096, 512], P(('groups', 'nodes', 'sub'), 'heads'), parts along dimension 0, may hold values from -6 to 6
- out_weight: bfloat16 [512, 512], P('heads'), may hold values from -0.25 to 0.25
- neighbours: int32 [32, 16], P('groups'), parts along dimension 0, may hold values from 0 to 15, as said below
- entry_mask: int32 [32, 16], P('groups'), parts along dimension 0, may hold values from 0 to 1, as said below
- live_counts: int32 [16], P('groups'), parts along dimension 0, may hold values from 1 to 2, as said below
- tile_slot: int32 [32], P('groups'), parts along dimension 0, may hold values from 0 to 15, as said below
Outputs:
- query_grad: bfloat16 [4096, 512], P(('groups', 'nodes', 'sub'), 'heads'), parts along dimension 0
- key_grad: bfloat16 [4096, 512], P(('groups', 'nodes', 'sub'), 'heads'), parts along dimension 0
- value_grad: bfloat16 [4096, 512], P(('groups', 'nodes', 'sub'), 'heads'), parts along dimension 0
- weight_grad: float32 [1024, 512], P(('groups', 'heads')), parts along dimension 0
There are 2 independent parts, one for each index of `groups`. A program takes and returns all parts, laid end to end along the dimension named above; an argument that names none is the same for every part. Nothing has to cross between parts.
Inputs may be any that keep to these rules, and one draw needn't show every extreme that they name: `neighbours`: row r lists graph tiles for the query tile in slot r. Entry 0 is that tile itself; entries 1 to 7 name live tiles of the same shard; entries 8 to 15 name live tiles of the shards next to it (shard index one lower or one higher, none past either end). Entries may repeat. Over all rows of one shard, the entries name at most one distinct tile of each adjacent shard, and in every draw some shard names exactly one tile of an adjacent shard. `entry_mask`: entry 0 of every row is 1. The live tiles of shard s are its slots s * 2 to s * 2 + live_counts[s] - 1; at least one shard is full. `tile_slot`: the graph tiles g with g // 2 = s are held in the slots of shard s, each slot once.
All inputs are finite; a program needn't handle non-finite values.
Results may differ from a plain program's by a relative error of at most 0.025.
Values may be sent and summed in bfloat16 or wider, within the bound.
A program may use at most 64 MiB of HBM per device.

v0:
```python
import jax
import jax.numpy as jnp
from jax import lax
from jax.sharding import PartitionSpec as P

HD = 64
TILE = 128


def extended(cells, sides, width):
    for axis, dim in sides:
        count = lax.axis_size(axis)
        ends = count - 1
        head = lax.slice_in_dim(cells, 0, width, axis=dim)
        tail = lax.slice_in_dim(cells, cells.shape[dim] - width, cells.shape[dim], axis=dim)
        cells = jnp.concatenate(
            [
                lax.ppermute(tail, axis, [(i, (i + 1) % count) for i in range(ends)]),
                cells,
                lax.ppermute(head, axis, [((i + 1) % count, i) for i in range(ends)]),
            ],
            axis=dim,
        )
    return cells


def passed_along(value, axis, steps):
    count = lax.axis_size(axis)
    first, last = (max(0, -steps), min(count, count - steps))
    return lax.ppermute(value, axis, [(source, source + steps) for source in range(first, last)])


def tile_terms(query_block, grad_block, key_tiles, value_tiles, usable, living, head_size):
    block_count, tile_rows, feature_width = query_block.shape
    head_count = feature_width // head_size
    entry_count = key_tiles.shape[1]
    scaling = head_size ** (-0.5)
    query_heads = query_block.reshape(block_count, tile_rows, head_count, head_size)
    grad_heads = grad_block.reshape(block_count, tile_rows, head_count, head_size)
    key_heads = key_tiles.reshape(block_count, entry_count, tile_rows, head_count, head_size)
    value_heads = value_tiles.reshape(block_count, entry_count, tile_rows, head_count, head_size)
    scores = (
        jnp.einsum("athd,aeshd->ahtes", query_heads, key_heads, preferred_element_type=jnp.float32)
        * scaling
    )
    visible = usable[:, None, None, :, None]
    scores = jnp.where(visible, scores, -1e30)
    topmost = jnp.max(scores, axis=(3, 4), keepdims=True)
    expanded = jnp.where(visible, jnp.exp(scores - topmost), 0.0)
    denominator = jnp.sum(expanded, axis=(3, 4), keepdims=True)
    denominator = jnp.where(living[:, None, None, None, None], denominator, 1.0)
    weights = expanded / denominator
    rounded = weights.astype(jnp.bfloat16)
    attended = jnp.einsum(
        "ahtes,aeshd->athd", rounded, value_heads, preferred_element_type=jnp.float32
    ).astype(jnp.bfloat16)
    row_delta = jnp.sum(grad_heads.astype(jnp.float32) * attended.astype(jnp.float32), axis=3)
    grad_scores = jnp.einsum(
        "athd,aeshd->ahtes", grad_heads, value_heads, preferred_element_type=jnp.float32
    )
    score_grad = (
        weights * (grad_scores - jnp.transpose(row_delta, (0, 2, 1))[:, :, :, None, None]) * scaling
    )
    score_half = score_grad.astype(jnp.bfloat16)
    query_part = jnp.einsum(
        "ahtes,aeshd->athd", score_half, key_heads, preferred_element_type=jnp.float32
    )
    key_part = jnp.einsum(
        "ahtes,athd->aeshd", score_half, query_heads, preferred_element_type=jnp.float32
    )
    value_part = jnp.einsum(
        "ahtes,athd->aeshd", rounded, grad_heads, preferred_element_type=jnp.float32
    )
    node_rows = block_count * tile_rows
    pair_rows = block_count * entry_count
    return (
        query_part.reshape(node_rows, feature_width),
        attended.reshape(node_rows, feature_width),
        key_part.reshape(pair_rows, tile_rows * feature_width),
        value_part.reshape(pair_rows, tile_rows * feature_width),
    )


def on_device(
    queries,
    key_vectors,
    value_vectors,
    cotangent,
    out_weight,
    neighbours,
    entry_mask,
    live_counts,
    tile_slot,
):
    row_count, feature_width = queries.shape
    tile_count = row_count // TILE
    heads_here = feature_width // HD
    shard_count = lax.axis_size(("nodes", "sub"))
    shard_index = lax.axis_index(("nodes", "sub"))
    gathered = lax.all_gather(cotangent, "heads", axis=1, tiled=True)
    out_grad = jnp.einsum(
        "nc,ic->ni", gathered, out_weight, preferred_element_type=jnp.float32
    ).astype(jnp.bfloat16)
    own_lists = lax.dynamic_slice_in_dim(neighbours, shard_index * tile_count, tile_count, 0)
    own_masks = lax.dynamic_slice_in_dim(entry_mask, shard_index * tile_count, tile_count, 0)
    live_count = lax.dynamic_index_in_dim(live_counts, shard_index, 0, keepdims=False)
    living = jnp.arange(tile_count, dtype=jnp.int32) < live_count
    usable = (own_masks == 1) & living[:, None]
    key_slot = jnp.take(tile_slot, own_lists)
    key_local = key_slot % tile_count
    offset = key_slot // tile_count - shard_index
    stacked = jnp.stack([key_vectors, value_vectors])
    window = extended(stacked, ((("nodes", "sub"), 1),), row_count)
    key_bank = window.reshape(2, 3 * tile_count, TILE, feature_width)
    bank_index = (offset + 1) * tile_count + key_local
    bank_size = key_bank.shape[1]
    block_tiles = max(
        (
            divisor
            for divisor in range(1, tile_count + 1)
            if tile_count % divisor == 0 and divisor * heads_here <= 4
        ),
        default=1,
    )
    partials = jnp.zeros((2, bank_size, TILE * feature_width), jnp.float32)
    query_parts = []
    attended_parts = []
    for first_tile in range(0, tile_count, block_tiles):
        last_tile = first_tile + block_tiles
        entry_bank = bank_index[first_tile:last_tile]
        key_tiles = jnp.take(key_bank[0], entry_bank, axis=0)
        value_tiles = jnp.take(key_bank[1], entry_bank, axis=0)
        query_block = queries[first_tile * TILE : last_tile * TILE].reshape(
            block_tiles, TILE, feature_width
        )
        grad_block = out_grad[first_tile * TILE : last_tile * TILE].reshape(
            block_tiles, TILE, feature_width
        )
        query_part, attended_part, key_part, value_part = tile_terms(
            query_block,
            grad_block,
            key_tiles,
            value_tiles,
            usable[first_tile:last_tile],
            living[first_tile:last_tile],
            HD,
        )
        partials = partials.at[:, entry_bank.reshape(-1)].add(jnp.stack([key_part, value_part]))
        query_parts.append(query_part)
        attended_parts.append(attended_part)
    query_grad = jnp.concatenate(query_parts, axis=0).astype(jnp.bfloat16)
    attended = jnp.concatenate(attended_parts, axis=0)
    middle = partials[:, tile_count : tile_count + tile_count]
    from_upper = passed_along(partials[:, :tile_count], ("nodes", "sub"), -1)
    from_lower = passed_along(partials[:, 2 * tile_count :], ("nodes", "sub"), 1)
    summed = middle + from_upper + from_lower
    key_grad = summed[0].reshape(row_count, feature_width).astype(jnp.bfloat16)
    value_grad = summed[1].reshape(row_count, feature_width).astype(jnp.bfloat16)
    weight_part = jnp.einsum("nf,nc->fc", attended, gathered, preferred_element_type=jnp.float32)
    weight_grad = lax.psum(weight_part, ("nodes", "sub")) * (row_count * shard_count) ** (-0.5)
    return (query_grad, key_grad, value_grad, weight_grad)


def solution(mesh):
    return jax.shard_map(
        on_device,
        mesh=mesh,
        in_specs=(
            P(("groups", "nodes", "sub"), "heads"),
            P(("groups", "nodes", "sub"), "heads"),
            P(("groups", "nodes", "sub"), "heads"),
            P(("groups", "nodes", "sub"), "heads"),
            P("heads", None),
            P("groups", None),
            P("groups", None),
            P("groups"),
            P("groups"),
        ),
        out_specs=(
            P(("groups", "nodes", "sub"), "heads"),
            P(("groups", "nodes", "sub"), "heads"),
            P(("groups", "nodes", "sub"), "heads"),
            P(("groups", "heads"), None),
        ),
        check_vma=False,
    )
```

profile of v0, /device:TPU:1, one launch (start us, length us, event | category | flops | bytes accessed | tf_op | source)
XLA Modules:
  0.0 177.3 jit_solution(18197746423502670191)
XLA Ops:
  8.3 1.9 %collective-permute-start.1 = (bf16[2,256,256]{2,1,0:T(8,128)(2,1)S(1)}, bf16[2,256,256]{2,1,0:T(8,128)(2,1)S(1)}, u32[]{:S(2)}, u32[]{:S(2)}) collective-permute-start(bf16[2,256,256]{2,1,0:T(8,128)(2,1)S(1)} %pad_maximum_fusion.1), channel_id=1, source_target_pairs={{1,0},{4,1},{5,4},{8,5},{9,8},{12,9},{13,12},{3,2},{6,3},{7,6},{10... | collective-permute-start | bytes 786440 | tf_op jit(solution)/shard_map/ppermute | solution.py:20
  10.2 4.6 %collective-permute-start = (bf16[2,256,256]{2,1,0:T(8,128)(2,1)S(1)}, bf16[2,256,256]{2,1,0:T(8,128)(2,1)S(1)}, u32[]{:S(2)}, u32[]{:S(2)}) collective-permute-start(bf16[2,256,256]{2,1,0:T(8,128)(2,1)S(1)} %pad_maximum_fusion.1), channel_id=1, source_target_pairs={{0,1},{1,4},{4,5},{5,8},{8,9},{9,12},{12,13},{2,3},{3,6},{6,7},{7,... | collective-permute-start | bytes 786440 | tf_op jit(solution)/shard_map/ppermute | solution.py:18
  22.4 5.4 %all_gather.3 = bf16[256,512]{1,0:T(8,128)(2,1)S(1)} all-gather(bf16[256,256]{1,0:T(8,128)(2,1)} %param.14), channel_id=1, replica_groups=mesh['groups'=2,'nodes'=4,'heads'=2,'sub'=2] {'heads'}, dimensions={1}, use_global_device_ids=true | all-gather | bytes 393216 | tf_op jit(solution)/shard_map/all_gather | solution.py:100
  34.6 2.8 %bitcast_select_fusion.2 = (bf16[1,16,128,256]{3,2,1,0:T(8,128)(2,1)}, bf16[1,16,128,256]{3,2,1,0:T(8,128)(2,1)}) fusion(bf16[16,128,256]{2,1,0:T(8,128)(2,1)} %gather_fusion.2, pred[16]{0:T(512)(128)(4,1)S(1)} %get-tuple-element.17, bf16[16,128,256]{2,1,0:T(8,128)(2,1)S(1)} %gather_fusion.1), kind=kLoop, calls=%fused_computation.48 | loop fusion | flops 1048576 | bytes 4194320 | tf_op jit(solution)/shard_map/jit(_take)/select_n | solution.py:132
  37.4 2.3 %copy.58 = bf16[1,16,128,256]{2,3,1,0:T(8,128)(2,1)} copy(bf16[1,16,128,256]{3,2,1,0:T(8,128)(2,1)} %get-tuple-element.25) | data formatting | bytes 2097152 | tf_op jit(solution)/shard_map/jit(_take)/select_n | solution.py:132
  46.8 2.4 %multiply_convert_fusion.1 = bf16[4,128,16,128]{1,3,2,0:T(8,128)(2,1)S(1)} fusion(bf16[128,4,64,1]{0,2,3,1:T(8,128)(2,1)S(1)} %bitcast.213, f32[4,128]{1,0:T(4,128)S(1)} %bitcast.218, bf16[16,128,4,64]{1,3,2,0:T(8,128)(2,1)S(1)} %bitcast.199, f32[4,128]{1,0:T(4,128)S(1)} %broadcast_select_fusion.1, f32[4,128]{1,0:T(4,128)S(1)} %get-tuple-element.33, ...), kind=kOutput, calls=%fused_computation.19 | convolution fusion | flops 143654912 | bytes 7411728 | tf_op jit(solution)/shard_map/athd,aeshd->ahtes/dot_general | solution.py:58
  50.3 2.2 %convolution_bitcast_fusion.3 = f32[1,16,128,4,64]{2,4,1,3,0:T(8,128)} fusion(bf16[4,128,16,128]{1,3,2,0:T(8,128)(2,1)S(1)} %multiply_convert_fusion.1, bf16[128,4,64,1]{0,2,3,1:T(8,128)(2,1)S(1)} %bitcast.207), kind=kOutput, calls=%fused_computation.36 | convolution fusion | flops 134217728 | bytes 4259840 | tf_op jit(solution)/shard_map/ahtes,athd->aeshd/dot_general | solution.py:68
  54.1 2.3 %copy.66 = bf16[1,16,128,256]{2,3,1,0:T(8,128)(2,1)} copy(bf16[1,16,128,256]{3,2,1,0:T(8,128)(2,1)} %get-tuple-element.27) | data formatting | bytes 2097152 | tf_op jit(solution)/shard_map/jit(_take)/select_n | solution.py:132
  58.0 4.8 %copy.74 = f32[1,16,128,4,64]{4,3,2,1,0:T(4,128)} copy(f32[1,16,128,4,64]{2,4,1,3,0:T(8,128)} %convolution_bitcast_fusion.3) | data formatting | bytes 4194304 | tf_op jit(solution)/shard_map/ahtes,athd->aeshd/transpose | solution.py:68
  62.8 5.6 %stack_reshape.12 = f32[1,16,32768]{2,1,0:T(8,128)} reshape(f32[1,16,128,4,64]{4,3,2,1,0:T(4,128)} %copy.74) | data formatting | bytes 4194304 | tf_op jit(solution)/shard_map/stack;reshape | solution.py:148
  68.4 3.1 %copy.76 = f32[1,16,128,4,64]{4,3,2,1,0:T(4,128)} copy(f32[1,16,128,4,64]{2,4,1,3,0:T(8,128)S(1)} %convolution_bitcast_fusion.2) | data formatting | bytes 4194304 | tf_op jit(solution)/shard_map/ahtes,athd->aeshd/transpose | solution.py:71
  71.5 5.7 %stack_reshape.13 = f32[1,16,32768]{2,1,0:T(8,128)} reshape(f32[1,16,128,4,64]{4,3,2,1,0:T(4,128)} %copy.76) | data formatting | bytes 4194304 | tf_op jit(solution)/shard_map/stack;reshape | solution.py:148
  79.2 5.2 %copy.77 = f32[16,2,32768]{2,1,0:T(2,128)} copy(f32[16,2,32768]{2,0,1:T(8,128)S(1)} %maximum_bitcast_fusion) | data formatting | bytes 8388608 | tf_op jit(solution)/shard_map/stack | solution.py:148
  89.8 2.4 %multiply_convert_fusion = bf16[4,128,16,128]{1,3,2,0:T(8,128)(2,1)S(1)} fusion(bf16[128,4,64,1]{0,2,3,1:T(8,128)(2,1)S(1)} %bitcast.210, f32[4,128]{1,0:T(4,128)S(1)} %bitcast.219, bf16[16,128,4,64]{1,3,2,0:T(8,128)(2,1)S(1)} %bitcast.195, f32[4,128]{1,0:T(4,128)S(1)} %broadcast_select_fusion, f32[4,128]{1,0:T(4,128)S(1)} %get-tuple-element.29, ...), kind=kOutput, calls=%fused_computation.17 | convolution fusion | flops 143654912 | bytes 7411728 | tf_op jit(solution)/shard_map/athd,aeshd->ahtes/dot_general | solution.py:58
  93.5 2.2 %convolution_bitcast_fusion.1 = f32[1,16,128,4,64]{2,4,1,3,0:T(8,128)} fusion(bf16[4,128,16,128]{1,3,2,0:T(8,128)(2,1)S(1)} %multiply_convert_fusion, bf16[128,4,64,1]{0,2,3,1:T(8,128)(2,1)S(1)} %bitcast.205), kind=kOutput, calls=%fused_computation.34 | convolution fusion | flops 134217728 | bytes 4259840 | tf_op jit(solution)/shard_map/ahtes,athd->aeshd/dot_general | solution.py:68
  96.7 4.8 %copy.79 = f32[1,16,128,4,64]{4,3,2,1,0:T(4,128)} copy(f32[1,16,128,4,64]{2,4,1,3,0:T(8,128)} %convolution_bitcast_fusion.1) | data formatting | bytes 4194304 | tf_op jit(solution)/shard_map/ahtes,athd->aeshd/transpose | solution.py:68
  101.5 5.6 %stack_reshape.14 = f32[1,16,32768]{2,1,0:T(8,128)} reshape(f32[1,16,128,4,64]{4,3,2,1,0:T(4,128)} %copy.79) | data formatting | bytes 4194304 | tf_op jit(solution)/shard_map/stack;reshape | solution.py:148
  107.1 3.2 %copy.81 = f32[1,16,128,4,64]{4,3,2,1,0:T(4,128)} copy(f32[1,16,128,4,64]{2,4,1,3,0:T(8,128)S(1)} %convolution_bitcast_fusion) | data formatting | bytes 4194304 | tf_op jit(solution)/shard_map/ahtes,athd->aeshd/transpose | solution.py:71
  110.3 5.7 %stack_reshape.15 = f32[1,16,32768]{2,1,0:T(8,128)} reshape(f32[1,16,128,4,64]{4,3,2,1,0:T(4,128)} %copy.81) | data formatting | bytes 4194304 | tf_op jit(solution)/shard_map/stack;reshape | solution.py:148
  117.9 5.2 %copy.82 = f32[16,2,32768]{2,1,0:T(2,128)} copy(f32[16,2,32768]{2,0,1:T(8,128)S(1)} %maximum_bitcast_fusion.1) | data formatting | bytes 8388608 | tf_op jit(solution)/shard_map/stack | solution.py:148
  123.5 14.6 %scatter_fusion = f32[2,6,32768]{2,0,1:T(2,128)S(1)} fusion(f32[2,6,32768]{2,0,1:T(2,128)S(1)} %broadcast_in_dim.106, s32[16]{0:T(128)S(1)} %get-tuple-element.16, f32[16,2,32768]{2,1,0:T(2,128)} %copy.77), kind=kCustom, calls=%fused_computation.5 | custom fusion | flops 1048576 | bytes 12582976 | tf_op jit(solution)/shard_map/scatter-add | solution.py:148
  138.2 14.6 %scatter_fusion.1 = f32[2,6,32768]{2,0,1:T(2,128)S(1)} fusion(f32[2,6,32768]{2,0,1:T(2,128)S(1)} %scatter_fusion, s32[16]{0:T(128)S(1)} %get-tuple-element.15, f32[16,2,32768]{2,1,0:T(2,128)} %copy.82), kind=kCustom, calls=%fused_computation.6 | custom fusion | flops 1048576 | bytes 12582976 | tf_op jit(solution)/shard_map/scatter-add | solution.py:148
  155.8 4.1 %collective-permute-start.3 = (f32[2,2,32768]{2,0,1:T(2,128)}, f32[2,2,32768]{2,0,1:T(2,128)}, u32[]{:S(2)}, u32[]{:S(2)}) collective-permute-start(f32[2,2,32768]{2,0,1:T(2,128)} %get-tuple-element.8), channel_id=1, source_target_pairs={{0,1},{1,4},{4,5},{5,8},{8,9},{9,12},{12,13},{2,3},{3,6},{6,7},{7,... | collective-permute-start | bytes 1572872 | tf_op jit(solution)/shard_map/ppermute | solution.py:30
  159.8 2.1 %fusion.28 = bf16[4,64,128]{2,1,0:T(8,128)(2,1)S(1)} fusion(bf16[16,128,4,64]{1,3,2,0:T(8,128)(2,1)S(1)} %bitcast.193, bf16[4,128,16,128]{1,3,2,0:T(8,128)(2,1)} %copy-done.7), kind=kOutput, calls=%fused_computation.42 | convolution fusion | flops 134250496 | bytes 3211264 | tf_op jit(solution)/shard_map/ahtes,aeshd->athd/dot_general | solution.py:65
  (92 shorter events, 50.3 us)
Async XLA Ops:
  7.2 21.4 %copy-start = (bf16[256,512]{1,0:T(8,128)(2,1)S(1)}, bf16[256,512]{1,0:T(8,128)(2,1)}, u32[]{:S(2)}) copy-start(bf16[256,512]{1,0:T(8,128)(2,1)} %param.15) | copy-start | bytes 786436
  7.2 155.7 %all-reduce.2.cloned.1.call-start = ((), (), s32[]{:S(2)}) async-start(), calls=%async_computation | async-start | bytes 1048576 | tf_op jit(solution)/shard_map/psum | solution.py:160
  8.3 20.8 %collective-permute-start.1 = (bf16[2,256,256]{2,1,0:T(8,128)(2,1)S(1)}, bf16[2,256,256]{2,1,0:T(8,128)(2,1)S(1)}, u32[]{:S(2)}, u32[]{:S(2)}) collective-permute-start(bf16[2,256,256]{2,1,0:T(8,128)(2,1)S(1)} %pad_maximum_fusion.1), channel_id=1, source_target_pairs={{1,0},{4,1},{5,4},{8,5},{9,8},{12,9},{13,12},{3,2},{6,3},{7,6},{10... | collective-permute-start | bytes 786440 | tf_op jit(solution)/shard_map/ppermute | solution.py:20
  10.2 18.9 %collective-permute-start = (bf16[2,256,256]{2,1,0:T(8,128)(2,1)S(1)}, bf16[2,256,256]{2,1,0:T(8,128)(2,1)S(1)}, u32[]{:S(2)}, u32[]{:S(2)}) collective-permute-start(bf16[2,256,256]{2,1,0:T(8,128)(2,1)S(1)} %pad_maximum_fusion.1), channel_id=1, source_target_pairs={{0,1},{1,4},{4,5},{5,8},{8,9},{9,12},{12,13},{2,3},{3,6},{6,7},{7,... | collective-permute-start | bytes 786440 | tf_op jit(solution)/shard_map/ppermute | solution.py:18
  27.8 0.7 copy-start.5
  41.3 2.2 %copy-start.9 = (bf16[1,16,128,256]{2,3,1,0:T(8,128)(2,1)}, bf16[1,16,128,256]{2,3,1,0:T(8,128)(2,1)S(1)}, u32[]{:S(2)}) copy-start(bf16[1,16,128,256]{2,3,1,0:T(8,128)(2,1)S(1)} %copy.55) | copy-start | bytes 3145732
  44.1 2.1 %copy-start.11 = (bf16[1,16,128,256]{2,3,1,0:T(8,128)(2,1)S(1)}, bf16[1,16,128,256]{2,3,1,0:T(8,128)(2,1)}, u32[]{:S(2)}) copy-start(bf16[1,16,128,256]{2,3,1,0:T(8,128)(2,1)} %copy.58) | copy-start | bytes 3145732
  46.8 2.4 %copy-start.10 = (bf16[1,16,128,256]{2,3,1,0:T(8,128)(2,1)S(1)}, bf16[1,16,128,256]{2,3,1,0:T(8,128)(2,1)}, u32[]{:S(2)}) copy-start(bf16[1,16,128,256]{2,3,1,0:T(8,128)(2,1)} %copy-done.9) | copy-start | bytes 3145732
  49.1 3.4 %copy-start.4 = (bf16[16,128,256]{2,1,0:T(8,128)(2,1)S(1)}, bf16[16,128,256]{2,1,0:T(8,128)(2,1)}, u32[]{:S(2)}) copy-start(bf16[16,128,256]{2,1,0:T(8,128)(2,1)} %gather_fusion.4) | copy-start | bytes 3145732
  49.2 3.3 %copy-start.13 = (pred[16]{0:T(512)(128)(4,1)S(1)}, pred[16]{0:T(512)(128)(4,1)}, u32[]{:S(2)}) copy-start(pred[16]{0:T(512)(128)(4,1)} %get-tuple-element.18) | copy-start | bytes 52
  71.5 5.8 %copy-start.2 = (f32[1,16,32768]{2,1,0:T(8,128)S(1)}, f32[1,16,32768]{2,1,0:T(8,128)}, u32[]{:S(2)}) copy-start(f32[1,16,32768]{2,1,0:T(8,128)} %stack_reshape.12) | copy-start | bytes 6291460
  87.1 2.1 %copy-start.8 = (bf16[1,16,128,256]{2,3,1,0:T(8,128)(2,1)S(1)}, bf16[1,16,128,256]{2,3,1,0:T(8,128)(2,1)}, u32[]{:S(2)}) copy-start(bf16[1,16,128,256]{2,3,1,0:T(8,128)(2,1)} %copy.66) | copy-start | bytes 3145732
  92.2 1.4 copy-start.7
  93.5 2.2 %copy-start.6 = (bf16[256,512]{1,0:T(8,128)(2,1)S(1)}, bf16[256,512]{1,0:T(8,128)(2,1)}, u32[]{:S(2)}) copy-start(bf16[256,512]{1,0:T(8,128)(2,1)} %copy-done.5) | copy-start | bytes 786436
  110.3 5.7 %copy-start.3 = (f32[1,16,32768]{2,1,0:T(8,128)S(1)}, f32[1,16,32768]{2,1,0:T(8,128)}, u32[]{:S(2)}) copy-start(f32[1,16,32768]{2,1,0:T(8,128)} %stack_reshape.14) | copy-start | bytes 6291460
  152.8 9.2 %copy-start.12 = (bf16[4,64,128]{2,1,0:T(8,128)(2,1)S(1)}, bf16[4,64,128]{2,1,0:T(8,128)(2,1)}, u32[]{:S(2)}) copy-start(bf16[4,64,128]{2,1,0:T(8,128)(2,1)} %fusion.34) | copy-start | bytes 196612
  152.8 17.7 %copy-start.1 = (bf16[256,512]{1,0:T(8,128)(2,1)S(1)}, bf16[256,512]{1,0:T(8,128)(2,1)}, u32[]{:S(2)}) copy-start(bf16[256,512]{1,0:T(8,128)(2,1)} %param.15) | copy-start | bytes 786436
  153.8 11.1 %collective-permute-start.2 = (f32[2,2,32768]{2,0,1:T(2,128)}, f32[2,2,32768]{2,0,1:T(2,128)S(1)}, u32[]{:S(2)}, u32[]{:S(2)}) collective-permute-start(f32[2,2,32768]{2,0,1:T(2,128)} %get-tuple-element.7), channel_id=1, source_target_pairs={{1,0},{4,1},{5,4},{8,5},{9,8},{12,9},{13,12},{3,2},{6,3},{7,6},{10... | collective-permute-start | bytes 1572872 | tf_op jit(solution)/shard_map/ppermute | solution.py:30
  155.8 10.5 %collective-permute-start.3 = (f32[2,2,32768]{2,0,1:T(2,128)}, f32[2,2,32768]{2,0,1:T(2,128)}, u32[]{:S(2)}, u32[]{:S(2)}) collective-permute-start(f32[2,2,32768]{2,0,1:T(2,128)} %get-tuple-element.8), channel_id=1, source_target_pairs={{0,1},{1,4},{4,5},{5,8},{8,9},{9,12},{12,13},{2,3},{3,6},{6,7},{7,... | collective-permute-start | bytes 1572872 | tf_op jit(solution)/shard_map/ppermute | solution.py:30
Sparse Core Ops, SparseCore 0:
  96.9 55.2 all-reduce.1
where the time goes:
time: 179 us; the launch traced here: 177 us
  local copies, waits for them, and re-layouts  72.2 us (40%)
  other arithmetic  52.8 us (29%)
  matrix products  18.4 us (10%)
  between operations  14.4 us (8%)
  starting transfers between devices  12.5 us (7%)
  blocking collectives  5.41 us (3%)
    another operation x6, local copies, waits for them, and re-layouts, on_device(): jnp.stack([key_part, value_part])  33 us
    scatter-add x2, other arithmetic, on_device(): partials.at[:, entry_bank.reshape(-1)]  29.2 us
    transpose x2, local copies, waits for them, and re-layouts, tile_terms(): jnp.einsum('ahtes,athd->aeshd', score_half, query_heads, preferred_elemen...  9.56 us
    transpose x2, local copies, waits for them, and re-layouts, tile_terms(): jnp.einsum('ahtes,athd->aeshd', rounded, grad_heads, preferred_element_ty...  6.31 us
    ppermute x2, starting transfers between devices, passed_along(): lax.ppermute(value, axis, [(source, source + steps) for source in range(f...  5.99 us
    all_gather x1, blocking collectives, on_device(): gathered = lax.all_gather(cotangent, 'heads', axis=1, tiled=True)  5.41 us
    dot_general x2, matrix products, tile_terms(): jnp.einsum('athd,aeshd->ahtes', grad_heads, value_heads, preferred_elemen...  4.7 us
    ppermute x1, starting transfers between devices, extended(): lax.ppermute(tail, axis, [(i, (i + 1) % count) for i in range(ends)])  4.58 us
  transfers between devices with their start and end apart: 5, of which 2 were waited for; matrix products, arithmetic and copies ran while one was open for 39% of the time, Pallas kernels for 0%

commit v1 on v0

v1 whole, which is shorter than its diff:
```python
import functools

import jax
import jax.numpy as jnp
from jax import lax
from jax.experimental import pallas as pl
from jax.experimental.pallas import tpu as pltpu
from jax.sharding import PartitionSpec as P

HD = 64
TILE = 128
LANES = 128
HIDDEN = -1e30
MESH = pl.DeviceIdType.MESH
F32 = jnp.float32
BF16 = jnp.bfloat16


def mm(a, b):
    return jnp.dot(a, b, preferred_element_type=F32)


def mm_nt(a, b):
    return lax.dot_general(a, b, (((1,), (1,)), ((), ())), preferred_element_type=F32)


def turned(value):
    return jnp.transpose(value.astype(F32))


def kernel(
    sizes,
    nb_ref, mask_ref, live_ref, slot_ref,
    q_ref, k_ref, v_ref, cot_ref, w_ref,
    dq_ref, dk_ref, dv_ref, wg_ref,
    cotg, hsend, halo, gsend, grecv, qt, qm, dot_t, dom, kt, vt, att, pf, pb, sb, wsend, wrecv, zsend, zrecv, ag,
    x_send, x_recv, h_send, h_recv, g_send, g_recv, p_send, p_recv, z_send, z_recv, a_send, a_recv, f_send, f_recv,
):
    nz, nx, ns, owners = sizes
    rows, feats = q_ref.shape
    tiles = rows // TILE
    heads = feats // HD
    pairs = feats // LANES
    per = LANES // HD
    shards = nz * ns
    half = feats // ns
    piece = half // owners
    degree = nb_ref.shape[1]
    total_nodes = rows * shards
    z, x, c = lax.axis_index("nodes"), lax.axis_index("heads"), lax.axis_index("sub")
    s = z * ns + c
    up, down = jnp.minimum(s + 1, shards - 1), jnp.maximum(s - 1, 0)
    has = (s > 0, s < shards - 1)
    sides = (down, up)

    def at_shard(index):
        return {"nodes": lax.div(index, ns), "sub": lax.rem(index, ns)}

    def on_x(d):
        return lax.rem(x + d, nx)

    def on_z(d):
        return lax.rem(z + d, nz)

    def on_sub(d):
        return lax.rem(c + d, ns)

    cross = (jnp.logical_and(c == 0, z > 0), jnp.logical_and(c == ns - 1, z < nz - 1))

    barrier = pltpu.get_barrier_semaphore()

    def greet(device):
        pl.semaphore_signal(barrier, inc=1, device_id=device, device_id_type=MESH)

    for d in range(1, nx):
        greet({"heads": on_x(d)})
    for d in range(1, ns):
        greet({"sub": on_sub(d)})
    for side in range(2):
        @pl.when(cross[side])
        def _():
            greet(at_shard(sides[side]))
    for d in range(1, nz):
        greet({"nodes": on_z(d)})

    chosen = []
    for side in range(2):
        pick = jnp.int32(0)
        for r in range(tiles):
            for e in range(degree):
                slot = slot_ref[nb_ref[sides[side] * tiles + r, e]]
                local = slot - s * tiles
                inside = jnp.logical_and(local >= 0, local < tiles)
                pick = jnp.where(inside, local, pick)
        chosen.append(pick)
    for side in range(2):
        kk, vv = k_ref[0:TILE, :], v_ref[0:TILE, :]
        for t in range(1, tiles):
            here = chosen[side] == t
            kk = jnp.where(here, k_ref[t * TILE : (t + 1) * TILE, :], kk)
            vv = jnp.where(here, v_ref[t * TILE : (t + 1) * TILE, :], vv)
        hsend[side, 0] = kk
        hsend[side, 1] = vv

    extra = jnp.where(jnp.logical_or(cross[0], cross[1]), 1, 0)
    pl.semaphore_wait(barrier, nx - 1 + ns - 1 + nz - 1 + extra)

    def remote(src, dst, send, recv, device):
        return pltpu.make_async_remote_copy(
            src_ref=src, dst_ref=dst, send_sem=send, recv_sem=recv, device_id=device, device_id_type=MESH
        )

    def halo_copy(side):
        return remote(hsend.at[side], halo.at[1 - side], h_send.at[side], h_recv.at[1 - side], at_shard(sides[side]))

    def halo_wait(side):
        return remote(hsend.at[side], halo.at[side], h_send.at[side], h_recv.at[side], at_shard(sides[side]))

    def grad_copy(side):
        return remote(gsend.at[side], grecv.at[1 - side], g_send.at[side], g_recv.at[1 - side], at_shard(sides[side]))

    def grad_wait(side):
        return remote(gsend.at[side], grecv.at[side], g_send.at[side], g_recv.at[side], at_shard(sides[side]))

    for side in range(2):
        @pl.when(has[side])
        def _():
            halo_copy(side).start()

    x_copies = [
        remote(cot_ref, cotg.at[x], x_send.at[d], x_recv.at[x], {"heads": on_x(d)}) for d in range(1, nx)
    ]
    for copy in x_copies:
        copy.start()
    for side in range(2):
        @pl.when(jnp.logical_not(has[side]))
        def _():
            halo[side] = jnp.zeros(halo.shape[1:], BF16)
            grecv[side] = jnp.zeros(grecv.shape[1:], BF16)
    cotg[x] = cot_ref[...]

    live = live_ref[s]
    counts = []
    for r in range(tiles):
        seen = [jnp.int32(0)] * (tiles + 2)
        for e in range(degree):
            local = slot_ref[nb_ref[s * tiles + r, e]] - s * tiles
            good = jnp.where(mask_ref[s * tiles + r, e] == 1, 1, 0)
            for t in range(tiles):
                seen[t] = seen[t] + jnp.where(local == t, good, 0)
            seen[tiles] = seen[tiles] + jnp.where(local < 0, good, 0)
            seen[tiles + 1] = seen[tiles + 1] + jnp.where(local >= tiles, good, 0)
        counts.append([jnp.where(r < live, n, 0) for n in seen])
    biases = [[jnp.where(n > 0, 0.0, HIDDEN).astype(F32) for n in row] for row in counts]
    counts = [[n.astype(F32) for n in row] for row in counts]

    scale = HD ** (-0.5)
    scaled = q_ref[...].astype(F32) * scale
    lane = lax.broadcasted_iota(jnp.int32, (rows, LANES), 1)
    sub_row = lax.broadcasted_iota(jnp.int32, (LANES, rows), 0)
    q_t = jnp.transpose(scaled)
    for h in range(heads):
        p, i = divmod(h, per)
        mine = jnp.logical_and(sub_row >= i * HD, sub_row < (i + 1) * HD)
        qt[h] = jnp.where(mine, q_t[p * LANES : (p + 1) * LANES, :], 0.0).astype(BF16)
        mine = jnp.logical_and(lane >= i * HD, lane < (i + 1) * HD)
        qm[h] = jnp.where(mine, scaled[:, p * LANES : (p + 1) * LANES], 0.0).astype(BF16)
    own = tiles * TILE
    keys = own + 2 * TILE
    kt[:, 0:own] = turned(k_ref[...]).astype(BF16)
    vt[:, 0:own] = turned(v_ref[...]).astype(BF16)
    for side in range(2):
        @pl.when(has[side])
        def _():
            halo_wait(side).wait_recv()
    for side in range(2):
        at = own + side * TILE
        kt[:, at : at + TILE] = turned(halo[side, 0]).astype(BF16)
        vt[:, at : at + TILE] = turned(halo[side, 1]).astype(BF16)

    for h in range(heads):
        p = h // per
        cols = slice(p * LANES, (p + 1) * LANES)
        blocks = [mm(k_ref[t * TILE : (t + 1) * TILE, cols], qt[h]) for t in range(tiles)]
        blocks += [mm(halo[side, 0, :, cols], qt[h]) for side in range(2)]
        for r in range(tiles):
            span = slice(r * TILE, (r + 1) * TILE)
            parts = [blocks[t][:, span] + biases[r][t] for t in range(tiles + 2)]
            top = functools.reduce(jnp.maximum, [jnp.max(part, axis=0, keepdims=True) for part in parts])
            parts = [jnp.exp(part - top) for part in parts]
            below = sum(jnp.sum(part, axis=0, keepdims=True) * counts[r][t] for t, part in enumerate(parts))
            below = jnp.where(below > 0.0, below, 1.0)
            for t, part in enumerate(parts):
                weight = part * (counts[r][t] / below)
                pf[h, t * TILE : (t + 1) * TILE, span] = weight
                pb[t * TILE : (t + 1) * TILE, h * rows + r * TILE : h * rows + (r + 1) * TILE] = weight.astype(BF16)
        att[h * HD : (h + 1) * HD, :] = mm(
            vt[h * HD : (h + 1) * HD, :], pb[:, h * rows : (h + 1) * rows]
        ).astype(BF16)

    for d in range(1, nx):
        remote(cot_ref, cotg.at[on_x(d)], x_send.at[d], x_recv.at[on_x(d)], {"heads": on_x(d)}).wait_recv()

    def weight_rows(index):
        lines = att[pl.ds(pl.multiple_of(index * half, half), half), :]
        return [mm(lines, cotg[i]) for i in range(nx)]

    p_copies = []
    for d in range(1, ns):
        for i, part in enumerate(weight_rows(on_sub(d))):
            wsend[d - 1, :, i * feats : (i + 1) * feats] = part.astype(BF16)
        copy = remote(wsend.at[d - 1], wrecv.at[d - 1], p_send.at[d], p_recv.at[d], {"sub": on_sub(d)})
        copy.start()
        p_copies.append(copy)
    mine_rows = weight_rows(c)

    dt = sum(mm_nt(w_ref[:, i * feats : (i + 1) * feats], cotg[i]) for i in range(nx)).astype(BF16)
    d_o = turned(dt)
    for h in range(heads):
        p, i = divmod(h, per)
        mine = jnp.logical_and(sub_row >= i * HD, sub_row < (i + 1) * HD)
        dot_t[h] = jnp.where(mine, dt[p * LANES : (p + 1) * LANES, :].astype(F32), 0.0).astype(BF16)
        mine = jnp.logical_and(lane >= i * HD, lane < (i + 1) * HD)
        dom[h] = jnp.where(mine, d_o[:, p * LANES : (p + 1) * LANES], 0.0).astype(BF16)
    product = dt.astype(F32) * att[...].astype(F32)
    deltas = [jnp.sum(product[h * HD : (h + 1) * HD, :], axis=0, keepdims=True) for h in range(heads)]

    for copy in p_copies:
        copy.wait_recv()
    chip = jnp.concatenate(mine_rows, axis=1)
    for d in range(1, ns):
        chip = chip + wrecv[d - 1].astype(F32)
    for j in range(owners):
        zsend[j] = chip[j * piece : (j + 1) * piece, :].astype(BF16)

    def piece_out(j):
        return remote(zsend.at[j], zrecv.at[z], z_send.at[j], z_recv.at[z], {"nodes": jnp.int32(j)})

    for j in range(owners):
        @pl.when(z != j)
        def _():
            piece_out(j).start()

    def score_grads(h, t, values):
        part = mm(values, dot_t[h])
        grad = pf[h, t * TILE : (t + 1) * TILE, :] * (part - deltas[h])
        sb[t * TILE : (t + 1) * TILE, h * rows : (h + 1) * rows] = grad.astype(BF16)

    def key_terms(t, p):
        area = slice(p * per * rows, (p + 1) * per * rows)
        lines = slice(t * TILE, (t + 1) * TILE)
        width = per * rows
        k_part = mm(sb[lines, area], qm[p * per : (p + 1) * per].reshape(width, LANES))
        v_part = mm(pb[lines, area], dom[p * per : (p + 1) * per].reshape(width, LANES))
        return k_part, v_part

    for side in range(2):
        for h in range(heads):
            cols = slice((h // per) * LANES, (h // per + 1) * LANES)
            score_grads(h, tiles + side, halo[side, 1, :, cols])
        for p in range(pairs):
            k_part, v_part = key_terms(tiles + side, p)
            gsend[side, 0, :, p * LANES : (p + 1) * LANES] = k_part.astype(BF16)
            gsend[side, 1, :, p * LANES : (p + 1) * LANES] = v_part.astype(BF16)

        @pl.when(has[side])
        def _():
            grad_copy(side).start()

    factor = total_nodes ** (-0.5)

    def piece_in(j):
        return remote(zsend.at[0], zrecv.at[j], z_send.at[0], z_recv.at[j], {"nodes": z})

    def owner_part():
        acc = zsend[z].astype(F32)
        for d in range(1, nz):
            j = on_z(d)
            piece_in(j).wait_recv()
            acc = acc + zrecv[j].astype(F32)
        ag[c, z] = (acc * factor).astype(BF16)
        for d in range(1, nz):
            remote(ag.at[c, z], ag.at[c, z], a_send.at[d], a_recv.at[z], {"nodes": on_z(d)}).start()
        for d in range(1, ns):
            remote(ag.at[c, z], ag.at[c, z], f_send.at[d - 1, z], f_recv.at[c, z], {"sub": on_sub(d)}).start()

    def forward_part(j):
        remote(ag.at[c, j], ag.at[c, j], a_send.at[0], a_recv.at[j], {"nodes": z}).wait_recv()
        for d in range(1, ns):
            remote(ag.at[c, j], ag.at[c, j], f_send.at[d - 1, j], f_recv.at[c, j], {"sub": on_sub(d)}).start()

    if owners == nz:
        owner_part()
    else:
        pl.when(z < owners)(owner_part)

    for t in range(tiles):
        for h in range(heads):
            cols = slice((h // per) * LANES, (h // per + 1) * LANES)
            score_grads(h, t, v_ref[t * TILE : (t + 1) * TILE, cols])
    own_terms = [[key_terms(t, p) for p in range(pairs)] for t in range(tiles)]
    dq_t = jnp.concatenate(
        [mm(kt[h * HD : (h + 1) * HD, :], sb[:, h * rows : (h + 1) * rows]) for h in range(heads)], axis=0
    )
    dq_ref[...] = (jnp.transpose(dq_t) * scale).astype(BF16)

    for j in range(owners):
        @pl.when(z != j)
        def _():
            forward_part(j)

    for side in range(2):
        @pl.when(has[side])
        def _():
            grad_wait(side).wait_recv()
    for t in range(tiles):
        lines = slice(t * TILE, (t + 1) * TILE)
        gates = [jnp.where(chosen[side] == t, 1.0, 0.0).astype(F32) for side in range(2)]
        for p in range(pairs):
            cols = slice(p * LANES, (p + 1) * LANES)
            for which, out in ((0, dk_ref), (1, dv_ref)):
                value = own_terms[t][p][which]
                for side in range(2):
                    value = value + grecv[side, which, :, cols].astype(F32) * gates[side]
                out[lines, cols] = value.astype(BF16)

    for d in range(1, ns):
        other = on_sub(d)
        for j in range(owners):
            remote(ag.at[c, j], ag.at[other, j], f_send.at[d - 1, j], f_recv.at[other, j], {"sub": other}).wait_recv()
    for i in range(ns):
        for j in range(owners):
            start = i * half + j * piece
            wg_ref[start : start + piece, :] = ag[i, j].astype(F32)

    for side in range(2):
        @pl.when(has[side])
        def _():
            halo_copy(side).wait_send()
            grad_copy(side).wait_send()
    for copy in x_copies:
        copy.wait_send()
    for copy in p_copies:
        copy.wait_send()
    for j in range(owners):
        @pl.when(z != j)
        def _():
            piece_out(j).wait_send()

    def owner_sent():
        for d in range(1, nz):
            remote(ag.at[c, z], ag.at[c, z], a_send.at[d], a_recv.at[z], {"nodes": on_z(d)}).wait_send()

    if owners == nz:
        owner_sent()
    else:
        pl.when(z < owners)(owner_sent)
    for d in range(1, ns):
        for j in range(owners):
            remote(ag.at[c, j], ag.at[c, j], f_send.at[d - 1, j], f_recv.at[c, j], {"sub": on_sub(d)}).wait_send()


def solution(mesh):
    nz, nx, ns = mesh.shape["nodes"], mesh.shape["heads"], mesh.shape["sub"]

    def on_device(
        queries, key_vectors, value_vectors, cotangent, out_weight, neighbours, entry_mask, live_counts, tile_slot
    ):
        rows, feats = queries.shape
        width = out_weight.shape[1]
        tiles, heads = rows // TILE, feats // HD
        keys = (tiles + 2) * TILE
        half = feats // ns
        owners = min(nz, half // 16)
        piece = half // owners
        vmem, smem = pl.BlockSpec(memory_space=pltpu.VMEM), pl.BlockSpec(memory_space=pltpu.SMEM)
        dma = pltpu.SemaphoreType.DMA
        return pl.pallas_call(
            functools.partial(kernel, (nz, nx, ns, owners)),
            out_shape=(
                jax.ShapeDtypeStruct((rows, feats), BF16),
                jax.ShapeDtypeStruct((rows, feats), BF16),
                jax.ShapeDtypeStruct((rows, feats), BF16),
                jax.ShapeDtypeStruct((feats, width), F32),
            ),
            in_specs=[smem] * 4 + [vmem] * 5,
            out_specs=(vmem,) * 4,
            scratch_shapes=[
                pltpu.VMEM((nx, rows, feats), BF16),
                pltpu.VMEM((2, 2, TILE, feats), BF16),
                pltpu.VMEM((2, 2, TILE, feats), BF16),
                pltpu.VMEM((2, 2, TILE, feats), BF16),
                pltpu.VMEM((2, 2, TILE, feats), BF16),
                pltpu.VMEM((heads, LANES, rows), BF16),
                pltpu.VMEM((heads, rows, LANES), BF16),
                pltpu.VMEM((heads, LANES, rows), BF16),
                pltpu.VMEM((heads, rows, LANES), BF16),
                pltpu.VMEM((feats, keys), BF16),
                pltpu.VMEM((feats, keys), BF16),
                pltpu.VMEM((feats, rows), BF16),
                pltpu.VMEM((heads, keys, rows), F32),
                pltpu.VMEM((keys, heads * rows), BF16),
                pltpu.VMEM((keys, heads * rows), BF16),
                pltpu.VMEM((ns - 1, half, width), BF16),
                pltpu.VMEM((ns - 1, half, width), BF16),
                pltpu.VMEM((owners, piece, width), BF16),
                pltpu.VMEM((nz, piece, width), BF16),
                pltpu.VMEM((ns, owners, piece, width), BF16),
                dma((nx,)), dma((nx,)),
                dma((2,)), dma((2,)),
                dma((2,)), dma((2,)),
                dma((ns,)), dma((ns,)),
                dma((owners,)), dma((nz,)),
                dma((nz,)), dma((owners,)),
                dma((ns - 1, owners)), dma((ns, owners)),
            ],
            compiler_params=pltpu.CompilerParams(
                collective_id=0, has_side_effects=True, vmem_limit_bytes=48 * 1024 * 1024
            ),
        )(neighbours, entry_mask, live_counts, tile_slot, queries, key_vectors, value_vectors, cotangent, out_weight)

    part = P(("groups", "nodes", "sub"), "heads")
    return jax.shard_map(
        on_device,
        mesh=mesh,
        in_specs=(
            part, part, part, part, P("heads", None), P("groups", None), P("groups", None), P("groups"), P("groups"),
        ),
        out_specs=(part, part, part, P(("groups", "heads"), None)),
        check_vma=False,
    )
```

time: 179 us -> 34.2 us (0.19)
  local copies, waits for them, and re-layouts: 72.2 us -> 10 us
  other arithmetic: 52.8 us -> 0 us
  Pallas kernels: 0 us -> 23.1 us
  matrix products: 18.4 us -> 0 us
  between operations: 14.4 us -> 0.66 us
  starting transfers between devices: 12.5 us -> 0 us
  blocking collectives: 5.41 us -> 0 us
    another operation x6 -> x0, local copies, waits for them, and re-layouts: 33 us -> none  [on_device(): jnp.stack([key_part, value_part])]
    scatter-add x2 -> x0, other arithmetic: 29.2 us -> none  [on_device(): partials.at[:, entry_bank.reshape(-1)]]
    pallas_call x0 -> x1, Pallas kernels: none -> 23.1 us  [on_device(): pl.pallas_call(functools.partial(kernel, (nz, nx, ns, owners)), out_shape...]
    dot_general x14 -> x0, matrix products: 18.4 us -> none  [the longest x2 4.7 us: tile_terms(): jnp.einsum('athd,aeshd->ahtes', grad_heads, value_heads, preferred_elemen...]
    transpose x4 -> x0, local copies, waits for them, and re-layouts: 15.9 us -> none  [the longest x2 9.56 us: tile_terms(): jnp.einsum('ahtes,athd->aeshd', score_half, query_heads, preferred_elemen...]
    ppermute x4 -> x0, starting transfers between devices: 12.5 us -> none  [the longest x2 5.99 us: passed_along(): lax.ppermute(value, axis, [(source, source + steps) for source in range(f...]
    unnamed x28 -> x22, local copies, waits for them, and re-layouts: 2.12 us -> 10 us
    select_n x4 -> x0, local copies, waits for them, and re-layouts: 7.79 us -> none  [the longest x2 4.57 us: on_device(): value_tiles = jnp.take(key_bank[1], entry_bank, axis=0)]
  transfers between devices with their start and end apart: 5 -> 0, of which waited for: 2 -> 0; matrix products, arithmetic and copies ran while one was open for 39% -> 0% of each run, Pallas kernels for 0% -> 0%
where the time goes in v1:
time: 34.2 us; the launch traced here: 33.8 us
  Pallas kernels  23.1 us (68%)
  local copies, waits for them, and re-layouts  10 us (29%)
  between operations  0.66 us (2%)
    pallas_call x1, Pallas kernels, on_device(): pl.pallas_call(functools.partial(kernel, (nz, nx, ns, owners)), out_shape...  23.1 us
    unnamed x22, local copies, waits for them, and re-layouts  10 us

profile of v1, /device:TPU:1, one launch (start us, length us, event | category | flops | bytes accessed | tf_op | source)
XLA Modules:
  0.0 33.8 jit_solution(1565707050566937593)
XLA Ops:
  0.6 0.0 copy-start
  0.6 0.9 %copy-done = bf16[256,512]{1,0:T(8,128)(2,1)S(1)} copy-done((bf16[256,512]{1,0:T(8,128)(2,1)S(1)}, bf16[256,512]{1,0:T(8,128)(2,1)}, u32[]{:S(2)}) %copy-start) | copy-done | bytes 262168
  1.6 0.0 copy-start.1
  1.6 0.9 %copy-done.1 = bf16[256,256]{1,0:T(8,128)(2,1)S(1)} copy-done((bf16[256,256]{1,0:T(8,128)(2,1)S(1)}, bf16[256,256]{1,0:T(8,128)(2,1)}, u32[]{:S(2)}) %copy-start.1) | copy-done | bytes 131096
  2.5 0.0 copy-start.2
  2.5 0.9 %copy-done.2 = bf16[256,256]{1,0:T(8,128)(2,1)S(1)} copy-done((bf16[256,256]{1,0:T(8,128)(2,1)S(1)}, bf16[256,256]{1,0:T(8,128)(2,1)}, u32[]{:S(2)}) %copy-start.2) | copy-done | bytes 131096
  3.4 0.0 copy-start.3
  3.4 0.9 %copy-done.3 = bf16[256,256]{1,0:T(8,128)(2,1)S(1)} copy-done((bf16[256,256]{1,0:T(8,128)(2,1)S(1)}, bf16[256,256]{1,0:T(8,128)(2,1)}, u32[]{:S(2)}) %copy-start.3) | copy-done | bytes 131096
  4.3 0.0 copy-start.4
  4.3 0.9 %copy-done.4 = bf16[256,256]{1,0:T(8,128)(2,1)S(1)} copy-done((bf16[256,256]{1,0:T(8,128)(2,1)S(1)}, bf16[256,256]{1,0:T(8,128)(2,1)}, u32[]{:S(2)}) %copy-start.4) | copy-done | bytes 131096
  5.2 0.0 copy-start.5
  5.2 0.7 %copy-done.5 = s32[16,16]{1,0:T(8,128)S(1)} copy-done((s32[16,16]{1,0:T(8,128)S(1)}, s32[16,16]{1,0:T(8,128)}, u32[]{:S(2)}) %copy-start.5) | copy-done | bytes 1048
  5.9 0.0 copy-start.6
  5.9 0.7 %copy-done.6 = s32[16,16]{1,0:T(8,128)S(1)} copy-done((s32[16,16]{1,0:T(8,128)S(1)}, s32[16,16]{1,0:T(8,128)}, u32[]{:S(2)}) %copy-start.6) | copy-done | bytes 1048
  6.6 0.0 copy-start.7
  6.6 0.7 %copy-done.7 = s32[8]{0:T(128)S(1)} copy-done((s32[8]{0:T(128)S(1)}, s32[8]{0:T(128)}, u32[]{:S(2)}) %copy-start.7) | copy-done | bytes 56
  7.3 0.0 copy-start.8
  7.3 0.7 %copy-done.8 = s32[16]{0:T(128)S(1)} copy-done((s32[16]{0:T(128)S(1)}, s32[16]{0:T(128)}, u32[]{:S(2)}) %copy-start.8) | copy-done | bytes 88
  7.9 23.1 %shard_map.120 = (bf16[256,256]{1,0:T(8,128)(2,1)S(1)}, bf16[256,256]{1,0:T(8,128)(2,1)S(1)}, bf16[256,256]{1,0:T(8,128)(2,1)S(1)}, f32[256,512]{1,0:T(8,128)S(1)}) custom-call(s32[16,16]{1,0:T(8,128)S(1)} %copy-done.5, s32[16,16]{1,0:T(8,128)S(1)} %copy-done.6, s32[8]{0:T(128)S(1)} %copy-done.7, s32[16]{0:T(128)S(1)} %copy-done.8, ...), custom_call_target="tpu_custom_call" | custom-call | tf_op jit(solution)/shard_map/pallas_call | solution.py:378
  31.0 0.7 %copy.17 = bf16[256,256]{1,0:T(8,128)(2,1)} copy(bf16[256,256]{1,0:T(8,128)(2,1)S(1)} %get-tuple-element.8) | data formatting | bytes 262144
  31.6 0.7 %copy.18 = bf16[256,256]{1,0:T(8,128)(2,1)} copy(bf16[256,256]{1,0:T(8,128)(2,1)S(1)} %get-tuple-element.9) | data formatting | bytes 262144
  32.3 0.7 %copy.19 = bf16[256,256]{1,0:T(8,128)(2,1)} copy(bf16[256,256]{1,0:T(8,128)(2,1)S(1)} %get-tuple-element.10) | data formatting | bytes 262144
  33.0 0.8 %copy.20 = f32[256,512]{1,0:T(8,128)} copy(f32[256,512]{1,0:T(8,128)S(1)} %get-tuple-element.11) | data formatting | bytes 1048576
Async XLA Ops:
  0.6 1.0 %copy-start = (bf16[256,512]{1,0:T(8,128)(2,1)S(1)}, bf16[256,512]{1,0:T(8,128)(2,1)}, u32[]{:S(2)}) copy-start(bf16[256,512]{1,0:T(8,128)(2,1)} %w_ref.1) | copy-start | bytes 786436
  1.6 0.9 %copy-start.1 = (bf16[256,256]{1,0:T(8,128)(2,1)S(1)}, bf16[256,256]{1,0:T(8,128)(2,1)}, u32[]{:S(2)}) copy-start(bf16[256,256]{1,0:T(8,128)(2,1)} %q_ref.1) | copy-start | bytes 393220
  2.5 0.9 %copy-start.2 = (bf16[256,256]{1,0:T(8,128)(2,1)S(1)}, bf16[256,256]{1,0:T(8,128)(2,1)}, u32[]{:S(2)}) copy-start(bf16[256,256]{1,0:T(8,128)(2,1)} %k_ref.1) | copy-start | bytes 393220
  3.4 0.9 %copy-start.3 = (bf16[256,256]{1,0:T(8,128)(2,1)S(1)}, bf16[256,256]{1,0:T(8,128)(2,1)}, u32[]{:S(2)}) copy-start(bf16[256,256]{1,0:T(8,128)(2,1)} %v_ref.1) | copy-start | bytes 393220
  4.3 0.9 %copy-start.4 = (bf16[256,256]{1,0:T(8,128)(2,1)S(1)}, bf16[256,256]{1,0:T(8,128)(2,1)}, u32[]{:S(2)}) copy-start(bf16[256,256]{1,0:T(8,128)(2,1)} %cot_ref.1) | copy-start | bytes 393220
  5.2 0.7 %copy-start.5 = (s32[16,16]{1,0:T(8,128)S(1)}, s32[16,16]{1,0:T(8,128)}, u32[]{:S(2)}) copy-start(s32[16,16]{1,0:T(8,128)} %nb_ref.1) | copy-start | bytes 3076
  5.9 0.7 %copy-start.6 = (s32[16,16]{1,0:T(8,128)S(1)}, s32[16,16]{1,0:T(8,128)}, u32[]{:S(2)}) copy-start(s32[16,16]{1,0:T(8,128)} %mask_ref.1) | copy-start | bytes 3076
  6.6 0.7 %copy-start.7 = (s32[8]{0:T(128)S(1)}, s32[8]{0:T(128)}, u32[]{:S(2)}) copy-start(s32[8]{0:T(128)} %live_ref.1) | copy-start | bytes 100
  7.3 0.7 %copy-start.8 = (s32[16]{0:T(128)S(1)}, s32[16]{0:T(128)}, u32[]{:S(2)}) copy-start(s32[16]{0:T(128)} %slot_ref.1) | copy-start | bytes 196

commit v2 on v1

--- a/solution.py
+++ b/solution.py
@@ -30,9 +30,10 @@
 
 def kernel(
     sizes,
-    nb_ref, mask_ref, live_ref, slot_ref,
-    q_ref, k_ref, v_ref, cot_ref, w_ref,
+    nb_hbm, mask_hbm, live_hbm, slot_hbm,
+    q_hbm, k_hbm, v_hbm, cot_ref, w_hbm,
     dq_ref, dk_ref, dv_ref, wg_ref,
+    nb_ref, mask_ref, live_ref, slot_ref, q_ref, k_ref, v_ref, w_ref, in_sem,
     cotg, hsend, halo, gsend, grecv, qt, qm, dot_t, dom, kt, vt, att, pf, pb, sb, wsend, wrecv, zsend, zrecv, ag,
     x_send, x_recv, h_send, h_recv, g_send, g_recv, p_send, p_recv, z_send, z_recv, a_send, a_recv, f_send, f_recv,
 ):
@@ -67,6 +68,15 @@
 
     cross = (jnp.logical_and(c == 0, z > 0), jnp.logical_and(c == ns - 1, z < nz - 1))
 
+    def load(index):
+        return pltpu.make_async_copy(*incoming[index], in_sem.at[index])
+
+    incoming = (
+        (nb_hbm, nb_ref), (slot_hbm, slot_ref), (k_hbm, k_ref), (v_hbm, v_ref), (mask_hbm, mask_ref),
+        (live_hbm, live_ref), (q_hbm, q_ref), (cot_ref, cotg.at[x]), (w_hbm, w_ref),
+    )
+    for i in range(len(incoming)):
+        load(i).start()
     barrier = pltpu.get_barrier_semaphore()
 
     def greet(device):
@@ -83,6 +93,8 @@
     for d in range(1, nz):
         greet({"nodes": on_z(d)})
 
+    load(0).wait()
+    load(1).wait()
     chosen = []
     for side in range(2):
         pick = jnp.int32(0)
@@ -93,6 +105,8 @@
                 inside = jnp.logical_and(local >= 0, local < tiles)
                 pick = jnp.where(inside, local, pick)
         chosen.append(pick)
+    load(2).wait()
+    load(3).wait()
     for side in range(2):
         kk, vv = k_ref[0:TILE, :], v_ref[0:TILE, :]
         for t in range(1, tiles):
@@ -137,8 +151,9 @@
         def _():
             halo[side] = jnp.zeros(halo.shape[1:], BF16)
             grecv[side] = jnp.zeros(grecv.shape[1:], BF16)
-    cotg[x] = cot_ref[...]
-
+
+    load(4).wait()
+    load(5).wait()
     live = live_ref[s]
     counts = []
     for r in range(tiles):
@@ -155,6 +170,7 @@
     counts = [[n.astype(F32) for n in row] for row in counts]
 
     scale = HD ** (-0.5)
+    load(6).wait()
     scaled = q_ref[...].astype(F32) * scale
     lane = lax.broadcasted_iota(jnp.int32, (rows, LANES), 1)
     sub_row = lax.broadcasted_iota(jnp.int32, (LANES, rows), 0)
@@ -198,6 +214,8 @@
             vt[h * HD : (h + 1) * HD, :], pb[:, h * rows : (h + 1) * rows]
         ).astype(BF16)
 
+    load(7).wait()
+    load(8).wait()
     for d in range(1, nx):
         remote(cot_ref, cotg.at[on_x(d)], x_send.at[d], x_recv.at[on_x(d)], {"heads": on_x(d)}).wait_recv()
 
@@ -331,7 +349,7 @@
     for i in range(ns):
         for j in range(owners):
             start = i * half + j * piece
-            wg_ref[start : start + piece, :] = ag[i, j].astype(F32)
+            wg_ref[start : start + piece, :] = ag[i, j]
 
     for side in range(2):
         @pl.when(has[side])
@@ -358,6 +376,21 @@
     for d in range(1, ns):
         for j in range(owners):
             remote(ag.at[c, j], ag.at[c, j], f_send.at[d - 1, j], f_recv.at[c, j], {"sub": on_sub(d)}).wait_send()
+
+
+def deliver(dq_ref, dk_ref, dv_ref, wg_ref, dq_out, dk_out, dv_out, wg_out, wide, sem):
+    copies = [
+        pltpu.make_async_copy(dq_ref, dq_out, sem.at[0]),
+        pltpu.make_async_copy(dk_ref, dk_out, sem.at[1]),
+        pltpu.make_async_copy(dv_ref, dv_out, sem.at[2]),
+        pltpu.make_async_copy(wide, wg_out, sem.at[3]),
+    ]
+    for copy in copies[:3]:
+        copy.start()
+    wide[...] = wg_ref[...].astype(F32)
+    copies[3].start()
+    for copy in copies:
+        copy.wait()
 
 
 def solution(mesh):
@@ -373,19 +406,28 @@
         half = feats // ns
         owners = min(nz, half // 16)
         piece = half // owners
-        vmem, smem = pl.BlockSpec(memory_space=pltpu.VMEM), pl.BlockSpec(memory_space=pltpu.SMEM)
+        vmem, hbm = pl.BlockSpec(memory_space=pltpu.VMEM), pl.BlockSpec(memory_space=pltpu.HBM)
         dma = pltpu.SemaphoreType.DMA
-        return pl.pallas_call(
+        partial = pl.pallas_call(
             functools.partial(kernel, (nz, nx, ns, owners)),
             out_shape=(
                 jax.ShapeDtypeStruct((rows, feats), BF16),
                 jax.ShapeDtypeStruct((rows, feats), BF16),
                 jax.ShapeDtypeStruct((rows, feats), BF16),
-                jax.ShapeDtypeStruct((feats, width), F32),
+                jax.ShapeDtypeStruct((feats, width), BF16),
             ),
-            in_specs=[smem] * 4 + [vmem] * 5,
+            in_specs=[hbm] * 9,
             out_specs=(vmem,) * 4,
             scratch_shapes=[
+                pltpu.SMEM(neighbours.shape, jnp.int32),
+                pltpu.SMEM(entry_mask.shape, jnp.int32),
+                pltpu.SMEM(live_counts.shape, jnp.int32),
+                pltpu.SMEM(tile_slot.shape, jnp.int32),
+                pltpu.VMEM((rows, feats), BF16),
+                pltpu.VMEM((rows, feats), BF16),
+                pltpu.VMEM((rows, feats), BF16),
+                pltpu.VMEM((feats, width), BF16),
+                dma((9,)),
                 pltpu.VMEM((nx, rows, feats), BF16),
                 pltpu.VMEM((2, 2, TILE, feats), BF16),
                 pltpu.VMEM((2, 2, TILE, feats), BF16),
@@ -417,7 +459,28 @@
             compiler_params=pltpu.CompilerParams(
                 collective_id=0, has_side_effects=True, vmem_limit_bytes=48 * 1024 * 1024
             ),
-        )(neighbours, entry_mask, live_counts, tile_slot, queries, key_vectors, value_vectors, cotangent, out_weight)
+        )(
+            *(
+                pltpu.with_memory_space_constraint(array, pltpu.HBM)
+                for array in (
+                    neighbours, entry_mask, live_counts, tile_slot,
+                    queries, key_vectors, value_vectors, cotangent, out_weight,
+                )
+            )
+        )
+        return pl.pallas_call(
+            deliver,
+            out_shape=(
+                jax.ShapeDtypeStruct((rows, feats), BF16),
+                jax.ShapeDtypeStruct((rows, feats), BF16),
+                jax.ShapeDtypeStruct((rows, feats), BF16),
+                jax.ShapeDtypeStruct((feats, width), F32),
+            ),
+            in_specs=[vmem] * 4,
+            out_specs=(hbm,) * 4,
+            scratch_shapes=[pltpu.VMEM((feats, width), F32), dma((4,))],
+            compiler_params=pltpu.CompilerParams(vmem_limit_bytes=4 * 1024 * 1024),
+        )(*partial)
 
     part = P(("groups", "nodes", "sub"), "heads")
     return jax.shard_map(

time: 34.2 us -> 24.3 us (0.71)
  local copies, waits for them, and re-layouts: 10 us -> 0 us
    unnamed x22 -> x0, local copies, waits for them, and re-layouts: 10 us -> none
    pallas_call x0 -> x1, Pallas kernels: none -> 0.96 us  [on_device(): pl.pallas_call(deliver, out_shape=(jax.ShapeDtypeStruct((rows, feats), BF...]
    pallas_call x1, Pallas kernels: 23.1 us -> 22.4 us  [on_device(): pl.pallas_call(functools.partial(kernel, (nz, nx, ns, owners)), out_shape...]
where the time goes in v2:
time: 24.3 us; the launch traced here: 24 us
  Pallas kernels  23.3 us (96%)
  between operations  0.64 us (3%)
    pallas_call x1, Pallas kernels, on_device(): pl.pallas_call(functools.partial(kernel, (nz, nx, ns, owners)), out_shape...  22.4 us
    pallas_call x1, Pallas kernels, on_device(): pl.pallas_call(deliver, out_shape=(jax.ShapeDtypeStruct((rows, feats), BF...  0.96 us

profile of v2, /device:TPU:1, one launch (start us, length us, event | category | flops | bytes accessed | tf_op | source)
XLA Modules:
  0.0 24.0 jit_solution(11367556885363288576)
XLA Ops:
  0.6 22.4 %shard_map.120 = (bf16[256,256]{1,0:T(8,128)(2,1)S(1)}, bf16[256,256]{1,0:T(8,128)(2,1)S(1)}, bf16[256,256]{1,0:T(8,128)(2,1)S(1)}, bf16[256,512]{1,0:T(8,128)(2,1)S(1)}) custom-call(s32[16,16]{1,0:T(8,128)} %nb_hbm.1, s32[16,16]{1,0:T(8,128)} %mask_hbm.1, s32[8]{0:T(128)} %live_hbm.1, s32[16]{0:T(128)} %slot_hbm.1, bf16[256,256]{1,0:T(8,128)(2,1)} %q_hbm.1, ...), custom_call_target="tpu_custom_call" | custom-call | tf_op jit(solution)/shard_map/pallas_call | solution.py:411
  23.0 1.0 %shard_map.121 = (bf16[256,256]{1,0:T(8,128)(2,1)}, bf16[256,256]{1,0:T(8,128)(2,1)}, bf16[256,256]{1,0:T(8,128)(2,1)}, f32[256,512]{1,0:T(8,128)}) custom-call(bf16[256,256]{1,0:T(8,128)(2,1)S(1)} %get-tuple-element.8.dq_ref, bf16[256,256]{1,0:T(8,128)(2,1)S(1)} %get-tuple-element.9.dk_ref, bf16[256,256]{1,0:T(8,128)(2,1)S(1)} %get-tuple-element.10.dv_ref, ...), custom_call_target="tpu_custom_call" | custom-call | tf_op jit(solution)/shard_map/pallas_call | solution.py:471

commit v3 on v2

--- a/solution.py
+++ b/solution.py
@@ -34,7 +34,7 @@
     q_hbm, k_hbm, v_hbm, cot_ref, w_hbm,
     dq_ref, dk_ref, dv_ref, wg_ref,
     nb_ref, mask_ref, live_ref, slot_ref, q_ref, k_ref, v_ref, w_ref, in_sem,
-    cotg, hsend, halo, gsend, grecv, qt, qm, dot_t, dom, kt, vt, att, pf, pb, sb, wsend, wrecv, zsend, zrecv, ag,
+    cotg, hsend, halo, gsend, grecv, qt, qm, dot_t, dom, kt, vt, att, pf, pb, sb, wsend, wrecv, zsend, zrecv, ag, stat,
     x_send, x_recv, h_send, h_recv, g_send, g_recv, p_send, p_recv, z_send, z_recv, a_send, a_recv, f_send, f_recv,
 ):
     nz, nx, ns, owners = sizes
@@ -185,6 +185,20 @@
     keys = own + 2 * TILE
     kt[:, 0:own] = turned(k_ref[...]).astype(BF16)
     vt[:, 0:own] = turned(v_ref[...]).astype(BF16)
+    for h in range(heads):
+        cols = slice((h // per) * LANES, (h // per + 1) * LANES)
+        blocks = [mm(k_ref[t * TILE : (t + 1) * TILE, cols], qt[h]) for t in range(tiles)]
+        for r in range(tiles):
+            span = slice(r * TILE, (r + 1) * TILE)
+            parts = [blocks[t][:, span] + biases[r][t] for t in range(tiles)]
+            top = functools.reduce(jnp.maximum, [jnp.max(part, axis=0, keepdims=True) for part in parts])
+            parts = [jnp.exp(part - top) for part in parts]
+            stat[0, h, :, span] = top
+            stat[1, h, :, span] = sum(
+                jnp.sum(part, axis=0, keepdims=True) * counts[r][t] for t, part in enumerate(parts)
+            )
+            for t, part in enumerate(parts):
+                pf[h, t * TILE : (t + 1) * TILE, span] = part
     for side in range(2):
         @pl.when(has[side])
         def _():
@@ -194,44 +208,78 @@
         kt[:, at : at + TILE] = turned(halo[side, 0]).astype(BF16)
         vt[:, at : at + TILE] = turned(halo[side, 1]).astype(BF16)
 
-    for h in range(heads):
-        p = h // per
-        cols = slice(p * LANES, (p + 1) * LANES)
-        blocks = [mm(k_ref[t * TILE : (t + 1) * TILE, cols], qt[h]) for t in range(tiles)]
-        blocks += [mm(halo[side, 0, :, cols], qt[h]) for side in range(2)]
+    def attend(h):
+        cols = pl.ds(pl.multiple_of(lax.div(h, per) * LANES, LANES), LANES)
+        blocks = [mm(halo[side, 0, :, cols], qt[h]) for side in range(2)]
         for r in range(tiles):
             span = slice(r * TILE, (r + 1) * TILE)
-            parts = [blocks[t][:, span] + biases[r][t] for t in range(tiles + 2)]
-            top = functools.reduce(jnp.maximum, [jnp.max(part, axis=0, keepdims=True) for part in parts])
+            into = pl.ds(pl.multiple_of(h * rows + r * TILE, TILE), TILE)
+            parts = [blocks[side][:, span] + biases[r][tiles + side] for side in range(2)]
+            before = stat[0, h, :, span]
+            top = functools.reduce(jnp.maximum, [jnp.max(part, axis=0, keepdims=True) for part in parts], before)
             parts = [jnp.exp(part - top) for part in parts]
-            below = sum(jnp.sum(part, axis=0, keepdims=True) * counts[r][t] for t, part in enumerate(parts))
-            below = jnp.where(below > 0.0, below, 1.0)
-            for t, part in enumerate(parts):
-                weight = part * (counts[r][t] / below)
-                pf[h, t * TILE : (t + 1) * TILE, span] = weight
-                pb[t * TILE : (t + 1) * TILE, h * rows + r * TILE : h * rows + (r + 1) * TILE] = weight.astype(BF16)
-        att[h * HD : (h + 1) * HD, :] = mm(
-            vt[h * HD : (h + 1) * HD, :], pb[:, h * rows : (h + 1) * rows]
-        ).astype(BF16)
-
+            shrink = jnp.exp(before - top)
+            below = stat[1, h, :, span] * shrink + sum(
+                jnp.sum(part, axis=0, keepdims=True) * counts[r][tiles + side] for side, part in enumerate(parts)
+            )
+            over = 1.0 / jnp.where(below > 0.0, below, 1.0)
+            for t in range(tiles + 2):
+                lines = slice(t * TILE, (t + 1) * TILE)
+                if t < tiles:
+                    weight = pf[h, lines, span] * (counts[r][t] * shrink * over)
+                else:
+                    weight = parts[t - tiles] * (counts[r][t] * over)
+                pf[h, lines, span] = weight
+                pb[lines, into] = weight.astype(BF16)
+        lines = pl.ds(pl.multiple_of(h * HD, HD), HD)
+        att[lines, :] = mm(vt[lines, :], pb[:, pl.ds(pl.multiple_of(h * rows, rows), rows)]).astype(BF16)
+
+    def weight_rows(index, i):
+        return mm(att[pl.ds(pl.multiple_of(index * half, half), half), :], cotg[on_x(i)])
+
+    def pair_copy(d, i):
+        return remote(
+            wsend.at[d - 1, i], wrecv.at[d - 1, i], p_send.at[d - 1, i], p_recv.at[d - 1, i], {"sub": on_sub(d)}
+        )
+
+    def pair_start(d, i):
+        wsend[d - 1, i] = weight_rows(on_sub(d), i).astype(BF16)
+        pair_copy(d, i).start()
+
+    here = heads // ns
     load(7).wait()
+    for d in range(1, ns):
+        for i in range(here):
+            attend(on_sub(d) * here + i)
+        pair_start(d, 0)
+    for i in range(here):
+        attend(c * here + i)
+    mine_rows = [weight_rows(c, 0)]
     load(8).wait()
     for d in range(1, nx):
         remote(cot_ref, cotg.at[on_x(d)], x_send.at[d], x_recv.at[on_x(d)], {"heads": on_x(d)}).wait_recv()
-
-    def weight_rows(index):
-        lines = att[pl.ds(pl.multiple_of(index * half, half), half), :]
-        return [mm(lines, cotg[i]) for i in range(nx)]
-
-    p_copies = []
-    for d in range(1, ns):
-        for i, part in enumerate(weight_rows(on_sub(d))):
-            wsend[d - 1, :, i * feats : (i + 1) * feats] = part.astype(BF16)
-        copy = remote(wsend.at[d - 1], wrecv.at[d - 1], p_send.at[d], p_recv.at[d], {"sub": on_sub(d)})
-        copy.start()
-        p_copies.append(copy)
-    mine_rows = weight_rows(c)
-
+    for i in range(1, nx):
+        for d in range(1, ns):
+            pair_start(d, i)
+        mine_rows.append(weight_rows(c, i))
+
+    def piece_out(i, j):
+        return remote(zsend.at[i, j], zrecv.at[i, z], z_send.at[i, j], z_recv.at[i, z], {"nodes": jnp.int32(j)})
+
+    def spread(i):
+        for d in range(1, ns):
+            pair_copy(d, i).wait_recv()
+        chip = mine_rows[i]
+        for d in range(1, ns):
+            chip = chip + wrecv[d - 1, i].astype(F32)
+        for j in range(owners):
+            zsend[i, j] = chip[j * piece : (j + 1) * piece, :].astype(BF16)
+        for j in range(owners):
+            @pl.when(z != j)
+            def _():
+                piece_out(i, j).start()
+
+    spread(0)
     dt = sum(mm_nt(w_ref[:, i * feats : (i + 1) * feats], cotg[i]) for i in range(nx)).astype(BF16)
     d_o = turned(dt)
     for h in range(heads):
@@ -242,23 +290,8 @@
         dom[h] = jnp.where(mine, d_o[:, p * LANES : (p + 1) * LANES], 0.0).astype(BF16)
     product = dt.astype(F32) * att[...].astype(F32)
     deltas = [jnp.sum(product[h * HD : (h + 1) * HD, :], axis=0, keepdims=True) for h in range(heads)]
-
-    for copy in p_copies:
-        copy.wait_recv()
-    chip = jnp.concatenate(mine_rows, axis=1)
-    for d in range(1, ns):
-        chip = chip + wrecv[d - 1].astype(F32)
-    for j in range(owners):
-        zsend[j] = chip[j * piece : (j + 1) * piece, :].astype(BF16)
-
-    def piece_out(j):
-        return remote(zsend.at[j], zrecv.at[z], z_send.at[j], z_recv.at[z], {"nodes": jnp.int32(j)})
-
-    for j in range(owners):
-        @pl.when(z != j)
-        def _():
-            piece_out(j).start()
-
+    for i in range(1, nx):
+        spread(i)
     def score_grads(h, t, values):
         part = mm(values, dot_t[h])
         grad = pf[h, t * TILE : (t + 1) * TILE, :] * (part - deltas[h])
@@ -287,25 +320,32 @@
 
     factor = total_nodes ** (-0.5)
 
-    def piece_in(j):
-        return remote(zsend.at[0], zrecv.at[j], z_send.at[0], z_recv.at[j], {"nodes": z})
+    def piece_in(i, j):
+        return remote(zsend.at[i, 0], zrecv.at[i, j], z_send.at[i, 0], z_recv.at[i, j], {"nodes": z})
+
+    def to_owner_peer(i, d):
+        return remote(ag.at[i, c, z], ag.at[i, c, z], a_send.at[i, d], a_recv.at[i, z], {"nodes": on_z(d)})
+
+    def to_core(i, j, d):
+        return remote(ag.at[i, c, j], ag.at[i, c, j], f_send.at[i, d - 1, j], f_recv.at[i, c, j], {"sub": on_sub(d)})
 
     def owner_part():
-        acc = zsend[z].astype(F32)
-        for d in range(1, nz):
-            j = on_z(d)
-            piece_in(j).wait_recv()
-            acc = acc + zrecv[j].astype(F32)
-        ag[c, z] = (acc * factor).astype(BF16)
-        for d in range(1, nz):
-            remote(ag.at[c, z], ag.at[c, z], a_send.at[d], a_recv.at[z], {"nodes": on_z(d)}).start()
+        for i in range(nx):
+            acc = zsend[i, z].astype(F32)
+            for d in range(1, nz):
+                j = on_z(d)
+                piece_in(i, j).wait_recv()
+                acc = acc + zrecv[i, j].astype(F32)
+            ag[i, c, z] = (acc * factor).astype(BF16)
+            for d in range(1, nz):
+                to_owner_peer(i, d).start()
+            for d in range(1, ns):
+                to_core(i, z, d).start()
+
+    def forward_part(i, j):
+        remote(ag.at[i, c, j], ag.at[i, c, j], a_send.at[i, 0], a_recv.at[i, j], {"nodes": z}).wait_recv()
         for d in range(1, ns):
-            remote(ag.at[c, z], ag.at[c, z], f_send.at[d - 1, z], f_recv.at[c, z], {"sub": on_sub(d)}).start()
-
-    def forward_part(j):
-        remote(ag.at[c, j], ag.at[c, j], a_send.at[0], a_recv.at[j], {"nodes": z}).wait_recv()
-        for d in range(1, ns):
-            remote(ag.at[c, j], ag.at[c, j], f_send.at[d - 1, j], f_recv.at[c, j], {"sub": on_sub(d)}).start()
+            to_core(i, j, d).start()
 
     if owners == nz:
         owner_part()
@@ -322,10 +362,6 @@
     )
     dq_ref[...] = (jnp.transpose(dq_t) * scale).astype(BF16)
 
-    for j in range(owners):
-        @pl.when(z != j)
-        def _():
-            forward_part(j)
 
     for side in range(2):
         @pl.when(has[side])
@@ -342,15 +378,26 @@
                     value = value + grecv[side, which, :, cols].astype(F32) * gates[side]
                 out[lines, cols] = value.astype(BF16)
 
+    for i in range(nx):
+        for j in range(owners):
+            @pl.when(z != j)
+            def _():
+                forward_part(i, j)
+    for i in range(nx):
+        cols = pl.ds(pl.multiple_of(on_x(i) * feats, feats), feats)
+        for j in range(owners):
+            start = j * piece
+            wg_ref[pl.ds(pl.multiple_of(c * half + start, piece), piece), cols] = ag[i, c, j]
     for d in range(1, ns):
         other = on_sub(d)
-        for j in range(owners):
-            remote(ag.at[c, j], ag.at[other, j], f_send.at[d - 1, j], f_recv.at[other, j], {"sub": other}).wait_recv()
-    for i in range(ns):
-        for j in range(owners):
-            start = i * half + j * piece
-            wg_ref[start : start + piece, :] = ag[i, j]
-
+        for i in range(nx):
+            cols = pl.ds(pl.multiple_of(on_x(i) * feats, feats), feats)
+            for j in range(owners):
+                remote(
+                    ag.at[i, c, j], ag.at[i, other, j], f_send.at[i, d - 1, j], f_recv.at[i, other, j], {"sub": other}
+                ).wait_recv()
+                start = j * piece
+                wg_ref[pl.ds(pl.multiple_of(other * half + start, piece), piece), cols] = ag[i, other, j]
     for side in range(2):
         @pl.when(has[side])
         def _():
@@ -358,24 +405,27 @@
             grad_copy(side).wait_send()
     for copy in x_copies:
         copy.wait_send()
-    for copy in p_copies:
-        copy.wait_send()
-    for j in range(owners):
-        @pl.when(z != j)
-        def _():
-            piece_out(j).wait_send()
+    for i in range(nx):
+        for d in range(1, ns):
+            pair_copy(d, i).wait_send()
+        for j in range(owners):
+            @pl.when(z != j)
+            def _():
+                piece_out(i, j).wait_send()
 
     def owner_sent():
-        for d in range(1, nz):
-            remote(ag.at[c, z], ag.at[c, z], a_send.at[d], a_recv.at[z], {"nodes": on_z(d)}).wait_send()
+        for i in range(nx):
+            for d in range(1, nz):
+                to_owner_peer(i, d).wait_send()
 
     if owners == nz:
         owner_sent()
     else:
         pl.when(z < owners)(owner_sent)
-    for d in range(1, ns):
-        for j in range(owners):
-            remote(ag.at[c, j], ag.at[c, j], f_send.at[d - 1, j], f_recv.at[c, j], {"sub": on_sub(d)}).wait_send()
+    for i in range(nx):
+        for d in range(1, ns):
+            for j in range(owners):
+                to_core(i, j, d).wait_send()
 
 
 def deliver(dq_ref, dk_ref, dv_ref, wg_ref, dq_out, dk_out, dv_out, wg_out, wide, sem):
@@ -443,18 +493,19 @@
                 pltpu.VMEM((heads, keys, rows), F32),
                 pltpu.VMEM((keys, heads * rows), BF16),
                 pltpu.VMEM((keys, heads * rows), BF16),
-                pltpu.VMEM((ns - 1, half, width), BF16),
-                pltpu.VMEM((ns - 1, half, width), BF16),
-                pltpu.VMEM((owners, piece, width), BF16),
-                pltpu.VMEM((nz, piece, width), BF16),
-                pltpu.VMEM((ns, owners, piece, width), BF16),
+                pltpu.VMEM((ns - 1, nx, half, feats), BF16),
+                pltpu.VMEM((ns - 1, nx, half, feats), BF16),
+                pltpu.VMEM((nx, owners, piece, feats), BF16),
+                pltpu.VMEM((nx, nz, piece, feats), BF16),
+                pltpu.VMEM((nx, ns, owners, piece, feats), BF16),
+                pltpu.VMEM((2, heads, 1, rows), F32),
                 dma((nx,)), dma((nx,)),
                 dma((2,)), dma((2,)),
                 dma((2,)), dma((2,)),
-                dma((ns,)), dma((ns,)),
-                dma((owners,)), dma((nz,)),
-                dma((nz,)), dma((owners,)),
-                dma((ns - 1, owners)), dma((ns, owners)),
+                dma((ns - 1, nx)), dma((ns - 1, nx)),
+                dma((nx, owners)), dma((nx, nz)),
+                dma((nx, nz)), dma((nx, owners)),
+                dma((nx, ns - 1, owners)), dma((nx, ns, owners)),
             ],
             compiler_params=pltpu.CompilerParams(
                 collective_id=0, has_side_effects=True, vmem_limit_bytes=48 * 1024 * 1024

time: 24.3 us -> 23.2 us (0.955)
  Pallas kernels: 23.3 us -> 22.2 us
    pallas_call x1, Pallas kernels: 22.4 us -> 21.3 us  [on_device(): pl.pallas_call(functools.partial(kernel, (nz, nx, ns, owners)), out_shape...]
where the time goes in v3:
time: 23.2 us; the launch traced here: 22.9 us
  Pallas kernels  22.2 us (96%)
  between operations  0.64 us (3%)
    pallas_call x1, Pallas kernels, on_device(): pl.pallas_call(functools.partial(kernel, (nz, nx, ns, owners)), out_shape...  21.3 us
    pallas_call x1, Pallas kernels, on_device(): pl.pallas_call(deliver, out_shape=(jax.ShapeDtypeStruct((rows, feats), BF...  0.96 us

profile of v3, /device:TPU:1, one launch (start us, length us, event | category | flops | bytes accessed | tf_op | source)
XLA Modules:
  0.0 22.9 jit_solution(9697602283500998704)
XLA Ops:
  0.6 21.3 %shard_map.120 = (bf16[256,256]{1,0:T(8,128)(2,1)S(1)}, bf16[256,256]{1,0:T(8,128)(2,1)S(1)}, bf16[256,256]{1,0:T(8,128)(2,1)S(1)}, bf16[256,512]{1,0:T(8,128)(2,1)S(1)}) custom-call(s32[16,16]{1,0:T(8,128)} %nb_hbm.1, s32[16,16]{1,0:T(8,128)} %mask_hbm.1, s32[8]{0:T(128)} %live_hbm.1, s32[16]{0:T(128)} %slot_hbm.1, bf16[256,256]{1,0:T(8,128)(2,1)} %q_hbm.1, ...), custom_call_target="tpu_custom_call" | custom-call | tf_op jit(solution)/shard_map/pallas_call | solution.py:461
  21.9 1.0 %shard_map.121 = (bf16[256,256]{1,0:T(8,128)(2,1)}, bf16[256,256]{1,0:T(8,128)(2,1)}, bf16[256,256]{1,0:T(8,128)(2,1)}, f32[256,512]{1,0:T(8,128)}) custom-call(bf16[256,256]{1,0:T(8,128)(2,1)S(1)} %get-tuple-element.8.dq_ref, bf16[256,256]{1,0:T(8,128)(2,1)S(1)} %get-tuple-element.9.dk_ref, bf16[256,256]{1,0:T(8,128)(2,1)S(1)} %get-tuple-element.10.dv_ref, ...), custom_call_target="tpu_custom_call" | custom-call | tf_op jit(solution)/shard_map/pallas_call | solution.py:522

commit v4 on v3

--- a/solution.py
+++ b/solution.py
@@ -124,11 +124,17 @@
             src_ref=src, dst_ref=dst, send_sem=send, recv_sem=recv, device_id=device, device_id_type=MESH
         )
 
-    def halo_copy(side):
-        return remote(hsend.at[side], halo.at[1 - side], h_send.at[side], h_recv.at[1 - side], at_shard(sides[side]))
-
-    def halo_wait(side):
-        return remote(hsend.at[side], halo.at[side], h_send.at[side], h_recv.at[side], at_shard(sides[side]))
+    def halo_copy(side, which):
+        return remote(
+            hsend.at[side, which], halo.at[1 - side, which], h_send.at[side, which], h_recv.at[1 - side, which],
+            at_shard(sides[side]),
+        )
+
+    def halo_wait(side, which):
+        return remote(
+            hsend.at[side, which], halo.at[side, which], h_send.at[side, which], h_recv.at[side, which],
+            at_shard(sides[side]),
+        )
 
     def grad_copy(side):
         return remote(gsend.at[side], grecv.at[1 - side], g_send.at[side], g_recv.at[1 - side], at_shard(sides[side]))
@@ -136,10 +142,11 @@
     def grad_wait(side):
         return remote(gsend.at[side], grecv.at[side], g_send.at[side], g_recv.at[side], at_shard(sides[side]))
 
-    for side in range(2):
-        @pl.when(has[side])
-        def _():
-            halo_copy(side).start()
+    for which in range(2):
+        for side in range(2):
+            @pl.when(has[side])
+            def _():
+                halo_copy(side, which).start()
 
     x_copies = [
         remote(cot_ref, cotg.at[x], x_send.at[d], x_recv.at[x], {"heads": on_x(d)}) for d in range(1, nx)
@@ -202,12 +209,7 @@
     for side in range(2):
         @pl.when(has[side])
         def _():
-            halo_wait(side).wait_recv()
-    for side in range(2):
-        at = own + side * TILE
-        kt[:, at : at + TILE] = turned(halo[side, 0]).astype(BF16)
-        vt[:, at : at + TILE] = turned(halo[side, 1]).astype(BF16)
-
+            halo_wait(side, 0).wait_recv()
     def attend(h):
         cols = pl.ds(pl.multiple_of(lax.div(h, per) * LANES, LANES), LANES)
         blocks = [mm(halo[side, 0, :, cols], qt[h]) for side in range(2)]
@@ -231,6 +233,8 @@
                     weight = parts[t - tiles] * (counts[r][t] * over)
                 pf[h, lines, span] = weight
                 pb[lines, into] = weight.astype(BF16)
+
+    def collect(h):
         lines = pl.ds(pl.multiple_of(h * HD, HD), HD)
         att[lines, :] = mm(vt[lines, :], pb[:, pl.ds(pl.multiple_of(h * rows, rows), rows)]).astype(BF16)
 
@@ -248,12 +252,22 @@
 
     here = heads // ns
     load(7).wait()
+    order = [on_sub(d) * here + i for d in list(range(1, ns)) + [0] for i in range(here)]
+    for h in order:
+        attend(h)
+    for side in range(2):
+        @pl.when(has[side])
+        def _():
+            halo_wait(side, 1).wait_recv()
+    for side in range(2):
+        at = own + side * TILE
+        vt[:, at : at + TILE] = turned(halo[side, 1]).astype(BF16)
     for d in range(1, ns):
-        for i in range(here):
-            attend(on_sub(d) * here + i)
+        for h in order[(d - 1) * here : d * here]:
+            collect(h)
         pair_start(d, 0)
-    for i in range(here):
-        attend(c * here + i)
+    for h in order[(ns - 1) * here :]:
+        collect(h)
     mine_rows = [weight_rows(c, 0)]
     load(8).wait()
     for d in range(1, nx):
@@ -347,6 +361,9 @@
         for d in range(1, ns):
             to_core(i, j, d).start()
 
+    for side in range(2):
+        at = own + side * TILE
+        kt[:, at : at + TILE] = turned(halo[side, 0]).astype(BF16)
     if owners == nz:
         owner_part()
     else:
@@ -401,7 +418,8 @@
     for side in range(2):
         @pl.when(has[side])
         def _():
-            halo_copy(side).wait_send()
+            for which in range(2):
+                halo_copy(side, which).wait_send()
             grad_copy(side).wait_send()
     for copy in x_copies:
         copy.wait_send()
@@ -500,7 +518,7 @@
                 pltpu.VMEM((nx, ns, owners, piece, feats), BF16),
                 pltpu.VMEM((2, heads, 1, rows), F32),
                 dma((nx,)), dma((nx,)),
-                dma((2,)), dma((2,)),
+                dma((2, 2)), dma((2, 2)),
                 dma((2,)), dma((2,)),
                 dma((ns - 1, nx)), dma((ns - 1, nx)),
                 dma((nx, owners)), dma((nx, nz)),

time: 23.2 us -> 22.7 us (0.978)
  Pallas kernels: 22.2 us -> 21.7 us
    pallas_call x1, Pallas kernels: 21.3 us -> 20.7 us  [on_device(): pl.pallas_call(functools.partial(kernel, (nz, nx, ns, owners)), out_shape...]
where the time goes in v4:
time: 22.7 us; the launch traced here: 22.3 us
  Pallas kernels  21.7 us (96%)
  between operations  0.64 us (3%)
    pallas_call x1, Pallas kernels, on_device(): pl.pallas_call(functools.partial(kernel, (nz, nx, ns, owners)), out_shape...  20.7 us
    pallas_call x1, Pallas kernels, on_device(): pl.pallas_call(deliver, out_shape=(jax.ShapeDtypeStruct((rows, feats), BF...  0.96 us

profile of v4, /device:TPU:1, one launch (start us, length us, event | category | flops | bytes accessed | tf_op | source)
XLA Modules:
  0.0 22.3 jit_solution(2650744890228714984)
XLA Ops:
  0.6 20.7 %shard_map.120 = (bf16[256,256]{1,0:T(8,128)(2,1)S(1)}, bf16[256,256]{1,0:T(8,128)(2,1)S(1)}, bf16[256,256]{1,0:T(8,128)(2,1)S(1)}, bf16[256,512]{1,0:T(8,128)(2,1)S(1)}) custom-call(s32[16,16]{1,0:T(8,128)} %nb_hbm.1, s32[16,16]{1,0:T(8,128)} %mask_hbm.1, s32[8]{0:T(128)} %live_hbm.1, s32[16]{0:T(128)} %slot_hbm.1, bf16[256,256]{1,0:T(8,128)(2,1)} %q_hbm.1, ...), custom_call_target="tpu_custom_call" | custom-call | tf_op jit(solution)/shard_map/pallas_call | solution.py:479
  21.4 1.0 %shard_map.121 = (bf16[256,256]{1,0:T(8,128)(2,1)}, bf16[256,256]{1,0:T(8,128)(2,1)}, bf16[256,256]{1,0:T(8,128)(2,1)}, f32[256,512]{1,0:T(8,128)}) custom-call(bf16[256,256]{1,0:T(8,128)(2,1)S(1)} %get-tuple-element.8.dq_ref, bf16[256,256]{1,0:T(8,128)(2,1)S(1)} %get-tuple-element.9.dk_ref, bf16[256,256]{1,0:T(8,128)(2,1)S(1)} %get-tuple-element.10.dv_ref, ...), custom_call_target="tpu_custom_call" | custom-call | tf_op jit(solution)/shard_map/pallas_call | solution.py:540

commit v5 on v4

--- a/solution.py
+++ b/solution.py
@@ -277,8 +277,15 @@
             pair_start(d, i)
         mine_rows.append(weight_rows(c, i))
 
+    def along_z(act, limit, distances):
+        for distance in distances:
+            for j in (z + distance, z - distance):
+                pl.when(jnp.logical_and(j >= 0, j < limit))(functools.partial(act, j))
+
+    near, far = range(1, nz), range(nz - 1, 0, -1)
+
     def piece_out(i, j):
-        return remote(zsend.at[i, j], zrecv.at[i, z], z_send.at[i, j], z_recv.at[i, z], {"nodes": jnp.int32(j)})
+        return remote(zsend.at[i, j], zrecv.at[i, z], z_send.at[i, j], z_recv.at[i, z], {"nodes": j})
 
     def spread(i):
         for d in range(1, ns):
@@ -288,10 +295,7 @@
             chip = chip + wrecv[d - 1, i].astype(F32)
         for j in range(owners):
             zsend[i, j] = chip[j * piece : (j + 1) * piece, :].astype(BF16)
-        for j in range(owners):
-            @pl.when(z != j)
-            def _():
-                piece_out(i, j).start()
+        along_z(lambda j: piece_out(i, j).start(), owners, far)
 
     spread(0)
     dt = sum(mm_nt(w_ref[:, i * feats : (i + 1) * feats], cotg[i]) for i in range(nx)).astype(BF16)
@@ -337,8 +341,8 @@
     def piece_in(i, j):
         return remote(zsend.at[i, 0], zrecv.at[i, j], z_send.at[i, 0], z_recv.at[i, j], {"nodes": z})
 
-    def to_owner_peer(i, d):
-        return remote(ag.at[i, c, z], ag.at[i, c, z], a_send.at[i, d], a_recv.at[i, z], {"nodes": on_z(d)})
+    def to_owner_peer(i, j):
+        return remote(ag.at[i, c, z], ag.at[i, c, z], a_send.at[i, j], a_recv.at[i, z], {"nodes": j})
 
     def to_core(i, j, d):
         return remote(ag.at[i, c, j], ag.at[i, c, j], f_send.at[i, d - 1, j], f_recv.at[i, c, j], {"sub": on_sub(d)})
@@ -351,8 +355,7 @@
                 piece_in(i, j).wait_recv()
                 acc = acc + zrecv[i, j].astype(F32)
             ag[i, c, z] = (acc * factor).astype(BF16)
-            for d in range(1, nz):
-                to_owner_peer(i, d).start()
+            along_z(lambda j: to_owner_peer(i, j).start(), nz, far)
             for d in range(1, ns):
                 to_core(i, z, d).start()
 
@@ -396,10 +399,7 @@
                 out[lines, cols] = value.astype(BF16)
 
     for i in range(nx):
-        for j in range(owners):
-            @pl.when(z != j)
-            def _():
-                forward_part(i, j)
+        along_z(functools.partial(forward_part, i), owners, near)
     for i in range(nx):
         cols = pl.ds(pl.multiple_of(on_x(i) * feats, feats), feats)
         for j in range(owners):
@@ -426,15 +426,11 @@
     for i in range(nx):
         for d in range(1, ns):
             pair_copy(d, i).wait_send()
-        for j in range(owners):
-            @pl.when(z != j)
-            def _():
-                piece_out(i, j).wait_send()
+        along_z(lambda j: piece_out(i, j).wait_send(), owners, far)
 
     def owner_sent():
         for i in range(nx):
-            for d in range(1, nz):
-                to_owner_peer(i, d).wait_send()
+            along_z(lambda j: to_owner_peer(i, j).wait_send(), nz, far)
 
     if owners == nz:
         owner_sent()

time: 22.7 us -> 22.8 us (level)
  no operation moved by 1% of the time
where the time goes in v5:
time: 22.8 us; the launch traced here: 22.5 us
  Pallas kernels  21.8 us (96%)
  between operations  0.64 us (3%)
    pallas_call x1, Pallas kernels, on_device(): pl.pallas_call(functools.partial(kernel, (nz, nx, ns, owners)), out_shape...  20.9 us
    pallas_call x1, Pallas kernels, on_device(): pl.pallas_call(deliver, out_shape=(jax.ShapeDtypeStruct((rows, feats), BF...  0.96 us

profile of v5, /device:TPU:1, one launch (start us, length us, event | category | flops | bytes accessed | tf_op | source)
XLA Modules:
  0.0 22.5 jit_solution(12183649396334905975)
XLA Ops:
  0.6 20.9 %shard_map.120 = (bf16[256,256]{1,0:T(8,128)(2,1)S(1)}, bf16[256,256]{1,0:T(8,128)(2,1)S(1)}, bf16[256,256]{1,0:T(8,128)(2,1)S(1)}, bf16[256,512]{1,0:T(8,128)(2,1)S(1)}) custom-call(s32[16,16]{1,0:T(8,128)} %nb_hbm.1, s32[16,16]{1,0:T(8,128)} %mask_hbm.1, s32[8]{0:T(128)} %live_hbm.1, s32[16]{0:T(128)} %slot_hbm.1, bf16[256,256]{1,0:T(8,128)(2,1)} %q_hbm.1, ...), custom_call_target="tpu_custom_call" | custom-call | tf_op jit(solution)/shard_map/pallas_call | solution.py:475
  21.5 1.0 %shard_map.121 = (bf16[256,256]{1,0:T(8,128)(2,1)}, bf16[256,256]{1,0:T(8,128)(2,1)}, bf16[256,256]{1,0:T(8,128)(2,1)}, f32[256,512]{1,0:T(8,128)}) custom-call(bf16[256,256]{1,0:T(8,128)(2,1)S(1)} %get-tuple-element.8.dq_ref, bf16[256,256]{1,0:T(8,128)(2,1)S(1)} %get-tuple-element.9.dk_ref, bf16[256,256]{1,0:T(8,128)(2,1)S(1)} %get-tuple-element.10.dv_ref, ...), custom_call_target="tpu_custom_call" | custom-call | tf_op jit(solution)/shard_map/pallas_call | solution.py:536
